TPU v7x, 32 devices: a whole 2x2x4 slice. The times are simulated.
32 devices in a mesh: dp: 8 (over z, x), mp: 4 (over y, core).
Axes of the slice: x: 2, y: 2, z: 4, core: 2. Of those that a mesh axis runs over, the one named last changes fastest.
Arguments:
- tokens: bfloat16 [16384, 768], P(('dp', 'mp')), may hold values from -6 to 6
- lengths: int32 [8, 16], P('dp'), may hold values from 1 to 1024, 2048 in all within a row
- w_qkv: bfloat16 [768, 3, 768], P(None, None, 'mp'), may hold values from -0.21875 to 0.21875
- w_out: bfloat16 [768, 768], P('mp'), may hold values from -0.875 to 0.875
- w_gate_up: bfloat16 [768, 2, 3072], P(None, None, 'mp'), may hold values from -0.21875 to 0.21875
- w_down: bfloat16 [3072, 768], P('mp'), may hold values from -0.109375 to 0.109375
- ln1_scale: float32 [768], replicated, may hold values from 0.5 to 1.5
- ln1_shift: float32 [768], replicated, may hold values from -2 to 2
- ln2_scale: float32 [768], replicated, may hold values from 0.5 to 1.5
- ln2_shift: float32 [768], replicated, may hold values from -2 to 2
- cotangent: bfloat16 [16384, 768], P(('dp', 'mp')), may hold values from -6 to 6
Outputs:
- output: bfloat16 [16384, 768], P(('dp', 'mp'))
- d_tokens: bfloat16 [16384, 768], P(('dp', 'mp'))
- grad_w_qkv: float32 [768, 3, 768], P(None, None, 'mp')
- grad_w_out: float32 [768, 768], P('mp')
- grad_w_gate_up: float32 [768, 2, 3072], P(None, None, 'mp')
- grad_w_down: float32 [3072, 768], P('mp')
- grad_ln1_scale: float32 [768], P('mp')
- grad_ln1_shift: float32 [768], P('mp')
- grad_ln2_scale: float32 [768], P('mp')
- grad_ln2_shift: float32 [768], P('mp')
Inputs may be any that keep to these rules, and one draw needn't show every extreme that they name: The 16 lengths of each row sum to 2048, and each row's longest is exactly 1024.
All inputs are finite; a program needn't handle non-finite values.
Results may differ from a plain program's by a relative error of at most 0.024.
Values may be sent and summed in bfloat16 or wider, within the bound.
A program may use at most 192 MiB of HBM per device.

v0:
```python
import math

import jax
import jax.numpy as jnp
from jax import lax
from jax.sharding import PartitionSpec as P

D = 768
HEAD_DIM = 64
ROW_LEN = 2048


EPSILON = 1e-05


def layer_norm(values, scale, shift):
    centred = values - jnp.mean(values, axis=-1, keepdims=True)
    spread = jnp.mean(centred * centred, axis=-1, keepdims=True)
    return centred * lax.rsqrt(spread + EPSILON) * scale + shift


def swiglu(gate_val, up_val):
    return gate_val * jax.nn.sigmoid(gate_val) * up_val


def doc_layout(lengths_row):
    places = jnp.arange(ROW_LEN, dtype=jnp.int32)
    doc_ends = jnp.cumsum(lengths_row)
    seg_ids = jnp.sum((places[:, None] >= doc_ends[None, :]).astype(jnp.int32), axis=1)
    doc_starts = doc_ends - lengths_row
    one_hot = seg_ids[:, None] == jnp.arange(lengths_row.shape[0], dtype=jnp.int32)[None, :]
    first_pos = jnp.sum(jnp.where(one_hot, doc_starts[None, :], 0), axis=1)
    return (seg_ids, places - first_pos)


def rotary_tables(positions):
    angle_rate = jnp.exp(
        jnp.arange(HEAD_DIM // 2, dtype=jnp.float32) * (-2.0 * math.log(1000.0) / HEAD_DIM)
    )
    angles = positions.astype(jnp.float32)[..., None] * angle_rate
    cosine = jnp.concatenate([jnp.cos(angles), jnp.cos(angles)], axis=-1)[..., None, :]
    sine_val = jnp.concatenate([jnp.sin(angles), jnp.sin(angles)], axis=-1)[..., None, :]
    return (cosine, sine_val)


def rotate(values, cosine, sine_val):
    half_dim = values.shape[-1] // 2
    turned = jnp.concatenate([-values[..., half_dim:], values[..., :half_dim]], axis=-1)
    return values * cosine + turned * sine_val


def rotate_back(grads_in, cosine, sine_val):
    half_dim = grads_in.shape[-1] // 2
    scaled = grads_in * sine_val
    turned = jnp.concatenate([scaled[..., half_dim:], -scaled[..., :half_dim]], axis=-1)
    return grads_in * cosine + turned


def attend_row(queries, keys_all, values_all, seg_ids, block_rows):
    local_heads = queries.shape[1]
    scale_qk = 1.0 / math.sqrt(HEAD_DIM)

    def attend(pair):
        q_block, q_seg = pair
        scores = (
            jnp.einsum("qhd,khd->hqk", q_block, keys_all, preferred_element_type=jnp.float32)
            * scale_qk
        )
        scores = jnp.where((q_seg[:, None] == seg_ids[None, :])[None], scores, -1e30)
        row_top = jnp.max(scores, axis=-1, keepdims=True)
        exp_terms = jnp.exp(scores - row_top)
        totals = jnp.sum(exp_terms, axis=-1, keepdims=True)
        attention = (exp_terms / totals).astype(jnp.bfloat16)
        block_out = jnp.einsum(
            "hqk,khd->qhd", attention, values_all, preferred_element_type=jnp.float32
        )
        return (block_out.astype(jnp.bfloat16), (row_top + jnp.log(totals))[..., 0])

    block_count = ROW_LEN // block_rows
    outs, log_totals = lax.map(
        attend,
        (
            queries.reshape(block_count, block_rows, local_heads, HEAD_DIM),
            seg_ids.reshape(block_count, block_rows),
        ),
    )
    return (outs.reshape(ROW_LEN, local_heads, HEAD_DIM), log_totals)


def attend_back(queries, keys_all, values_all, seg_ids, log_totals, d_attended, block_rows):
    local_heads = queries.shape[1]
    scale_qk = 1.0 / math.sqrt(HEAD_DIM)
    block_count = ROW_LEN // block_rows

    def step_block(carry, pieces):
        d_keys, d_values = carry
        q_block, q_seg, lse_block, d_block = pieces
        scores = (
            jnp.einsum("qhd,khd->hqk", q_block, keys_all, preferred_element_type=jnp.float32)
            * scale_qk
        )
        allowed = (q_seg[:, None] == seg_ids[None, :])[None]
        attention = jnp.where(
            allowed, jnp.exp(jnp.where(allowed, scores, -1e30) - lse_block[..., None]), 0.0
        )
        d_probs = jnp.einsum(
            "qhd,khd->hqk", d_block, values_all, preferred_element_type=jnp.float32
        )
        row_dot = jnp.sum(attention * d_probs, axis=-1, keepdims=True)
        d_scores = (attention * (d_probs - row_dot)).astype(jnp.bfloat16)
        d_query = (
            jnp.einsum("hqk,khd->qhd", d_scores, keys_all, preferred_element_type=jnp.float32)
            * scale_qk
        )
        d_keys = (
            d_keys
            + jnp.einsum("hqk,qhd->khd", d_scores, q_block, preferred_element_type=jnp.float32)
            * scale_qk
        )
        d_values = d_values + jnp.einsum(
            "hqk,qhd->khd",
            attention.astype(jnp.bfloat16),
            d_block,
            preferred_element_type=jnp.float32,
        )
        return ((d_keys, d_values), d_query)

    zero_grad = jnp.zeros((ROW_LEN, local_heads, HEAD_DIM), jnp.float32)
    pieces = (
        queries.reshape(block_count, block_rows, local_heads, HEAD_DIM),
        seg_ids.reshape(block_count, block_rows),
        log_totals,
        d_attended.reshape(block_count, block_rows, local_heads, HEAD_DIM),
    )
    (d_keys, d_values), d_queries = lax.scan(step_block, (zero_grad, zero_grad), pieces)
    return (d_queries.reshape(ROW_LEN, local_heads, HEAD_DIM), d_keys, d_values)


def body(
    tokens,
    lengths,
    w_qkv,
    w_out,
    w_gate_up,
    w_down,
    ln1_scale,
    ln1_shift,
    ln2_scale,
    ln2_shift,
    cotangent,
):
    rows_here = lengths.shape[0]
    full_len = rows_here * ROW_LEN
    local_cols = w_out.shape[0]
    local_heads = local_cols // HEAD_DIM
    hidden_cols = w_down.shape[0]
    block_rows = min(512, ROW_LEN)
    contract_rows = (((0,), (0,)), ((), ()))
    contract_cols = (((1,), (1,)), ((), ()))
    seg_ids, positions = jax.vmap(doc_layout)(lengths)
    cosine, sine_val = rotary_tables(positions)
    gathered = lax.all_gather(tokens, "mp", axis=0, tiled=True)
    flat_qkv = w_qkv.reshape(D, 3 * local_cols)
    projected = jnp.dot(gathered, flat_qkv, preferred_element_type=jnp.float32)
    projected = projected.reshape(rows_here, ROW_LEN, 3, local_heads, HEAD_DIM)
    queries = rotate(projected[:, :, 0], cosine, sine_val).astype(jnp.bfloat16)
    keys_all = rotate(projected[:, :, 1], cosine, sine_val).astype(jnp.bfloat16)
    values_all = projected[:, :, 2].astype(jnp.bfloat16)
    attended, log_totals = lax.map(
        lambda group: attend_row(group[0], group[1], group[2], group[3], block_rows),
        (queries, keys_all, values_all, seg_ids),
    )
    attended_flat = attended.reshape(full_len, local_cols)
    branch = lax.psum_scatter(
        jnp.dot(attended_flat, w_out, preferred_element_type=jnp.float32).astype(jnp.bfloat16),
        "mp",
        scatter_dimension=0,
        tiled=True,
    ).astype(jnp.float32)
    normed, norm1_back = jax.vjp(
        layer_norm, tokens.astype(jnp.float32) + branch, ln1_scale, ln1_shift
    )
    normed_all = lax.all_gather(normed.astype(jnp.bfloat16), "mp", axis=0, tiled=True)
    flat_gate_up = w_gate_up.reshape(D, 2 * hidden_cols)
    gate_up = jnp.dot(normed_all, flat_gate_up, preferred_element_type=jnp.float32)
    hidden_full, act_back = jax.vjp(swiglu, gate_up[:, :hidden_cols], gate_up[:, hidden_cols:])
    hidden = hidden_full.astype(jnp.bfloat16)
    mlp_out = lax.psum_scatter(
        jnp.dot(hidden, w_down, preferred_element_type=jnp.float32).astype(jnp.bfloat16),
        "mp",
        scatter_dimension=0,
        tiled=True,
    ).astype(jnp.float32)
    output_full, norm2_back = jax.vjp(layer_norm, normed + mlp_out, ln2_scale, ln2_shift)
    output = output_full.astype(jnp.bfloat16)
    d_sum, d_scale_two, d_shift_two = norm2_back(cotangent.astype(jnp.float32))
    d_mlp_all = lax.all_gather(d_sum.astype(jnp.bfloat16), "mp", axis=0, tiled=True)
    d_hidden = lax.dot_general(d_mlp_all, w_down, contract_cols, preferred_element_type=jnp.float32)
    grad_down = lax.dot_general(
        hidden, d_mlp_all, contract_rows, preferred_element_type=jnp.float32
    )
    d_gate, d_up = act_back(d_hidden)
    d_gate_up = jnp.concatenate([d_gate.astype(jnp.bfloat16), d_up.astype(jnp.bfloat16)], axis=1)
    grad_gate_up = lax.dot_general(
        normed_all, d_gate_up, contract_rows, preferred_element_type=jnp.float32
    ).reshape(D, 2, hidden_cols)
    d_normed_part = lax.dot_general(
        d_gate_up, flat_gate_up, contract_cols, preferred_element_type=jnp.float32
    )
    norm2_grads = jnp.stack([d_scale_two, d_shift_two], axis=1)
    d_normed_piece, norm2_sum = (
        lax.psum_scatter(
            d_normed_part.astype(jnp.bfloat16), "mp", scatter_dimension=0, tiled=True
        ).astype(jnp.float32),
        lax.psum_scatter(
            norm2_grads.astype(jnp.bfloat16), "mp", scatter_dimension=0, tiled=True
        ).astype(jnp.float32),
    )
    d_resid, d_scale_one, d_shift_one = norm1_back(d_sum + d_normed_piece)
    d_attn_all = lax.all_gather(d_resid.astype(jnp.bfloat16), "mp", axis=0, tiled=True)
    grad_out = lax.dot_general(
        attended_flat, d_attn_all, contract_rows, preferred_element_type=jnp.float32
    )
    d_attended = lax.dot_general(
        d_attn_all, w_out, contract_cols, preferred_element_type=jnp.float32
    ).astype(jnp.bfloat16)
    d_attended = d_attended.reshape(rows_here, ROW_LEN, local_heads, HEAD_DIM)
    d_queries, d_keys, d_values = lax.map(
        lambda group: attend_back(
            group[0], group[1], group[2], group[3], group[4], group[5], block_rows
        ),
        (queries, keys_all, values_all, seg_ids, log_totals, d_attended),
    )
    d_projected = jnp.stack(
        [
            rotate_back(d_queries, cosine, sine_val).astype(jnp.bfloat16),
            rotate_back(d_keys, cosine, sine_val).astype(jnp.bfloat16),
            d_values.astype(jnp.bfloat16),
        ],
        axis=2,
    )
    d_projected = d_projected.reshape(full_len, 3 * local_cols)
    grad_qkv = lax.dot_general(
        gathered, d_projected, contract_rows, preferred_element_type=jnp.float32
    ).reshape(D, 3, local_cols)
    d_input_part = lax.dot_general(
        d_projected, flat_qkv, contract_cols, preferred_element_type=jnp.float32
    )
    norm1_grads = jnp.stack([d_scale_one, d_shift_one], axis=1)
    d_input_piece, norm1_sum = (
        lax.psum_scatter(
            d_input_part.astype(jnp.bfloat16), "mp", scatter_dimension=0, tiled=True
        ).astype(jnp.float32),
        lax.psum_scatter(
            norm1_grads.astype(jnp.bfloat16), "mp", scatter_dimension=0, tiled=True
        ).astype(jnp.float32),
    )
    d_tokens = (d_resid + d_input_piece).astype(jnp.bfloat16)
    grad_qkv, grad_out, grad_gate_up, grad_down, norm1_sum, norm2_sum = lax.psum(
        (grad_qkv, grad_out, grad_gate_up, grad_down, norm1_sum, norm2_sum), "dp"
    )
    return (
        output,
        d_tokens,
        grad_qkv,
        grad_out,
        grad_gate_up,
        grad_down,
        norm1_sum[:, 0],
        norm1_sum[:, 1],
        norm2_sum[:, 0],
        norm2_sum[:, 1],
    )


def solution(mesh):
    return jax.shard_map(
        body,
        mesh=mesh,
        in_specs=(
            P(("dp", "mp"), None),
            P("dp", None),
            P(None, None, "mp"),
            P("mp", None),
            P(None, None, "mp"),
            P("mp", None),
            P(),
            P(),
            P(),
            P(),
            P(("dp", "mp"), None),
        ),
        out_specs=(
            P(("dp", "mp"), None),
            P(("dp", "mp"), None),
            P(None, None, "mp"),
            P("mp", None),
            P(None, None, "mp"),
            P("mp", None),
            P("mp"),
            P("mp"),
            P("mp"),
            P("mp"),
        ),
        check_vma=False,
    )
```

profile of v0, /device:TPU:0, one launch (start us, length us, event | category | flops | bytes accessed | tf_op | source)
XLA Modules:
  0.0 964.4 jit_solution(18277112338146265710)
XLA Ops:
  13.8 27.1 %all-gather.5.cloned.1.call-done = bf16[2048,768]{1,0:T(8,128)(2,1)} async-done(((bf16[512,768]{1,0:T(8,128)(2,1)}), bf16[2048,768]{1,0:T(8,128)(2,1)}) %all-gather.5.cloned.1.call-update) | async-done | bytes 3145744 | tf_op jit(solution)/shard_map/all_gather | solution.py:162
  63.2 85.2 %while.47 = (s32[]{:T(128)}, bf16[4,512,3,64]{1,3,2,0:T(8,128)(2,1)}, f32[4,3,512]{2,1,0:T(4,128)}, s32[4,512]{1,0:T(4,128)S(1)}, s32[2048]{0:T(1024)S(1)}, /*in...) while((s32[]{:T(128)}, ...), condition=%wide.region_6.7_spmd, body=%wide.region_3.6_spmd.sunk | while | flops 844200448 | bytes 43975780 | solution.py:80
  63.9 6.0 fusion.124
  69.9 6.8 fusion.125
  77.2 7.3 fusion.126
  85.2 6.0 fusion.124
  91.2 6.8 fusion.125
  98.5 7.3 fusion.126
  106.5 6.0 fusion.124
  112.5 6.8 fusion.125
  119.8 7.3 fusion.126
  127.8 6.0 fusion.124
  133.8 6.8 fusion.125
  141.1 7.3 fusion.126
  154.7 38.1 %reduce-scatter.11.cloned.1.call-done = bf16[512,768]{1,0:T(8,128)(2,1)} async-done(((bf16[2048,768]{1,0:T(8,128)(2,1)}), bf16[512,768]{1,0:T(8,128)(2,1)}) %reduce-scatter.11.cloned.1.call-update) | async-done | bytes 786448 | tf_op jit(solution)/shard_map/reduce_scatter | solution.py:174
  202.7 24.9 %all-gather.7.cloned.1.call-done = bf16[2048,768]{1,0:T(8,128)(2,1)} async-done(((bf16[512,768]{1,0:T(8,128)(2,1)}), bf16[2048,768]{1,0:T(8,128)(2,1)}) %all-gather.7.cloned.1.call-update) | async-done | bytes 3145744 | tf_op jit(solution)/shard_map/all_gather | solution.py:183
  227.6 8.2 fusion.72
  246.1 38.1 %reduce-scatter.13.cloned.1.call-done = bf16[512,768]{1,0:T(8,128)(2,1)} async-done(((bf16[2048,768]{1,0:T(8,128)(2,1)}), bf16[512,768]{1,0:T(8,128)(2,1)}) %reduce-scatter.13.cloned.1.call-update) | async-done | bytes 786448 | tf_op jit(solution)/shard_map/reduce_scatter | solution.py:188
  292.0 28.3 %all-gather.9.cloned.1.call-done = bf16[2048,768]{1,0:T(8,128)(2,1)} async-done(((bf16[512,768]{1,0:T(8,128)(2,1)}), bf16[2048,768]{1,0:T(8,128)(2,1)}) %all-gather.9.cloned.1.call-update) | async-done | bytes 3145744 | tf_op jit(solution)/shard_map/all_gather | solution.py:197
  320.2 8.3 fusion.38
  331.2 6.5 fusion.42
  337.8 38.1 %reduce-scatter.15.cloned.1.call-done = bf16[512,768]{1,0:T(8,128)(2,1)} async-done(((bf16[2048,768]{1,0:T(8,128)(2,1)}), bf16[512,768]{1,0:T(8,128)(2,1)}) %reduce-scatter.15.cloned.1.call-update) | async-done | bytes 786448 | tf_op jit(solution)/shard_map/reduce_scatter | solution.py:212
  384.2 26.3 %all-gather.11.cloned.1.call-done = bf16[2048,768]{1,0:T(8,128)(2,1)} async-done(((bf16[512,768]{1,0:T(8,128)(2,1)}), bf16[2048,768]{1,0:T(8,128)(2,1)}) %all-gather.11.cloned.1.call-update) | async-done | bytes 3145744 | tf_op jit(solution)/shard_map/all_gather | solution.py:220
  419.8 167.2 %while.48 = (s32[]{:T(128)}, f32[2048,3,64]{0,2,1:T(8,128)S(1)}, f32[2048,3,64]{0,2,1:T(8,128)}, f32[4,512,3,64]{1,0,3,2:T(4,128)}, bf16[4,512,3,64]{1,3,2,0:T(8...) while((s32[]{:T(128)}, f32[2048,3,64]{0,2,1:T(8,128)S(1)}, ...), condition=%wide.region_20.21_spmd.clone, body=%wide.region_18.20_spmd.clone.sunk | while | flops 2047834624 | bytes 136231104 | solution.py:135
  423.9 8.8 multiply_reduce_fusion.6
  432.8 5.5 multiply_convert_fusion.4
  441.2 8.6 dynamic_update_slice.33
  449.9 4.3 fusion.137
  454.2 7.1 fusion.138
  465.5 8.8 multiply_reduce_fusion.6
  474.3 5.5 multiply_convert_fusion.4
  482.8 8.6 dynamic_update_slice.33
  495.7 7.5 fusion.138
  507.3 8.8 multiply_reduce_fusion.6
  516.2 5.5 multiply_convert_fusion.4
  524.6 8.6 dynamic_update_slice.33
  533.3 4.3 fusion.137
  537.5 7.5 fusion.138
  549.2 8.8 multiply_reduce_fusion.6
  558.0 5.5 multiply_convert_fusion.4
  566.5 8.6 dynamic_update_slice.33
  575.1 4.3 fusion.137
  579.4 7.5 fusion.138
  604.5 11.0 %fusion.40 = f32[768,1536]{1,0:T(8,128)} fusion(bf16[2048,768]{1,0:T(8,128)(2,1)} %all-gather.7.cloned.1.call-done, bf16[2048,768]{0,1:T(8,128)(2,1)} %copy-done.55, bf16[2048,768]{0,1:T(8,128)(2,1)} %copy-done.54), kind=kOutput, calls=%fused_computation.55 | convolution fusion | flops 4844421120 | bytes 14155776 | tf_op jit(solution)/shard_map/dot_general | solution.py:204
  615.6 6.9 reshape.613
  622.4 7.0 fusion.75
  636.3 21.7 %all-reduce = (f32[192,2]{0,1:T(2,128)S(1)}, f32[192,2]{0,1:T(2,128)S(1)}) all-reduce(bf16[192,2]{0,1:T(2,128)(2,1)S(1)} %copy.50, bf16[192,2]{0,1:T(2,128)(2,1)S(1)} %copy.52), channel_id=1, replica_groups=mesh['dp'=8,'mp'=4] {'dp'}, use_global_device_ids=true, to_apply=%region_29.30 | all-reduce | flops 768 | bytes 4608 | tf_op jit(solution)/shard_map/psum | solution.py:259
  661.4 286.5 %all-reduce.4.cloned.1.call-done = (f32[768,3,192]{0,2,1:T(8,128)}, f32[192,768]{1,0:T(8,128)}, f32[768,2,768]{2,1,0:T(2,128)}, f32[768,768]{1,0:T(8,128)}) async-done(((f32[768,3,192]{0,2,1:T(8,128)}, f32[192,768]{1,0:T(8,128)}, f32[768,2,768]{2,1,0:T(2,128)}, f32[768,768]{1,0:T(8,128)}), (f32[768,3,192]{0,2,1:T(8,128)}, f32[192,768]{1,0:T(8,128)}, f32[768,2,768]{2,1,0:T(2,128)}, ...) | async-done | bytes 9437200 | tf_op jit(solution)/shard_map/psum | solution.py:259
  (275 shorter events, 158.2 us)
Async XLA Ops:
  7.2 234.8 %copy-start = (bf16[768,768]{1,0:T(8,128)(2,1)S(1)}, bf16[768,768]{1,0:T(8,128)(2,1)}, u32[]{:S(2)}) copy-start(bf16[768,768]{1,0:T(8,128)(2,1)} %param.20) | copy-start | bytes 3538948
  7.2 33.7 %all-gather.5.cloned.1.call-start = ((), (), s32[]{:S(2)}) async-start(), calls=%async_computation.6 | async-start | bytes 3932160 | tf_op jit(solution)/shard_map/all_gather | solution.py:162
  7.9 184.8 %reduce-scatter.11.cloned.1.call-start = ((), (), s32[]{:S(2)}) async-start(), calls=%async_computation.7 | async-start | bytes 3932160 | tf_op jit(solution)/shard_map/reduce_scatter | solution.py:174
  13.8 45.5 %copy-start.15 = (f32[2048,64]{0,1:T(8,128)}, f32[2048,64]{0,1:T(8,128)S(1)}, u32[]{:S(2)}) copy-start(f32[2048,64]{0,1:T(8,128)S(1)} %get-tuple-element.331) | copy-start | bytes 1572868
  45.0 2.7 copy-start.20
  59.3 2.7 copy-start.25
  59.3 2.9 copy-start.26
  59.3 3.1 copy-start.34
  59.3 3.2 copy-start.35
  148.4 6.1 copy-start.24
  148.4 3.4 copy-start.36
  154.6 38.1 %copy-start.3 = (bf16[512,768]{1,0:T(8,128)(2,1)S(1)}, bf16[512,768]{1,0:T(8,128)(2,1)}, u32[]{:S(2)}) copy-start(bf16[512,768]{1,0:T(8,128)(2,1)} %param.15) | copy-start | bytes 2359300
  154.6 73.0 %all-gather.7.cloned.1.call-start = ((), (), s32[]{:S(2)}) async-start(), calls=%async_computation.8 | async-start | bytes 3932160 | tf_op jit(solution)/shard_map/all_gather | solution.py:183
  192.7 4.2 copy-start.7
  198.9 85.2 %reduce-scatter.13.cloned.1.call-start = ((), (), s32[]{:S(2)}) async-start(), calls=%async_computation.9 | async-start | bytes 3932160 | tf_op jit(solution)/shard_map/reduce_scatter | solution.py:188
  235.8 4.5 copy-start.12
  246.1 74.2 %all-gather.9.cloned.1.call-start = ((), (), s32[]{:S(2)}) async-start(), calls=%async_computation.10 | async-start | bytes 3932160 | tf_op jit(solution)/shard_map/all_gather | solution.py:197
  291.5 84.4 %reduce-scatter.15.cloned.1.call-start = ((), (), s32[]{:S(2)}) async-start(), calls=%async_computation.11 | async-start | bytes 3932160 | tf_op jit(solution)/shard_map/reduce_scatter | solution.py:212
  320.2 11.0 %copy-start.30 = (bf16[96,8,2,768]{3,1,2,0:T(8,128)(2,1)S(1)}, bf16[96,8,2,768]{3,1,2,0:T(8,128)(2,1)}, u32[]{:S(2)}) copy-start(bf16[96,8,2,768]{3,1,2,0:T(8,128)(2,1)} %copy.67) | copy-start | bytes 7077892
  328.6 2.7 copy-start.55
  337.7 38.2 %copy-start.39 = (f32[512]{0:T(512)S(1)}, f32[512]{0:T(512)}, u32[]{:S(2)}) copy-start(f32[512]{0:T(512)} %copy-done.38) | copy-start | bytes 6148
  337.7 38.2 %copy-start.40 = (f32[768]{0:T(1024)S(1)}, f32[768]{0:T(1024)}, u32[]{:S(2)}) copy-start(f32[768]{0:T(1024)} %param.21) | copy-start | bytes 9220
  337.7 38.2 %copy-start.42 = (f32[512]{0:T(512)S(1)}, f32[512]{0:T(512)}, u32[]{:S(2)}) copy-start(f32[512]{0:T(512)} %copy-done.41) | copy-start | bytes 6148
  337.7 38.2 %copy-start.44 = (f32[512]{0:T(512)S(1)}, f32[512]{0:T(512)}, u32[]{:S(2)}) copy-start(f32[512]{0:T(512)} %copy-done.43) | copy-start | bytes 6148
  337.7 40.9 %copy-start.46 = (f32[512]{0:T(512)S(1)}, f32[512]{0:T(512)}, u32[]{:S(2)}) copy-start(f32[512]{0:T(512)} %copy-done.45) | copy-start | bytes 6148
  337.8 72.8 %all-gather.11.cloned.1.call-start = ((), (), s32[]{:S(2)}) async-start(), calls=%async_computation.12 | async-start | bytes 3932160 | tf_op jit(solution)/shard_map/all_gather | solution.py:220
  375.9 2.8 copy-start.9
  375.9 2.8 copy-start.29
  379.7 4.3 copy-start.47
  380.8 29.8 %copy-start.37 = (bf16[192,768]{1,0:T(8,128)(2,1)S(1)}, bf16[192,768]{1,0:T(8,128)(2,1)}, u32[]{:S(2)}) copy-start(bf16[192,768]{1,0:T(8,128)(2,1)} %param.18) | copy-start | bytes 884740
  381.9 252.5 %reduce-scatter.21.cloned.1.call-start = ((), (), s32[]{:S(2)}) async-start(), calls=%async_computation.15 | async-start | bytes 245760
  383.1 252.4 %reduce-scatter.19.cloned.1.call-start = ((), (), s32[]{:S(2)}) async-start(), calls=%async_computation.14 | async-start | bytes 245760
  384.0 275.1 %reduce-scatter.17.cloned.1.call-start = ((), (), s32[]{:S(2)}) async-start(), calls=%async_computation.13 | async-start | bytes 3932160 | tf_op jit(solution)/shard_map/reduce_scatter | solution.py:251
  414.5 5.2 copy-start.5
  454.2 7.2 copy-start.6
  495.7 7.5 copy-start.6
  537.5 7.5 copy-start.6
  579.4 7.5 copy-start.6
  587.0 6.5 copy-start.17
  604.5 343.4 %all-reduce.4.cloned.1.call-start = ((), (), s32[]{:S(2)}) async-start(), calls=%async_computation.16 | async-start | bytes 18874368 | tf_op jit(solution)/shard_map/psum | solution.py:259
  622.4 7.0 copy-start.14
  622.4 7.0 copy-start.27
  622.4 8.7 copy-start.52
  634.4 24.8 %copy-start.11 = (f32[512,768]{1,0:T(8,128)S(1)}, f32[512,768]{1,0:T(8,128)}, u32[]{:S(2)}) copy-start(f32[512,768]{1,0:T(8,128)} %copy-done.10) | copy-start | bytes 4718596
  634.4 24.8 %copy-start.48 = (f32[512]{0:T(512)S(1)}, f32[512]{0:T(512)}, u32[]{:S(2)}) copy-start(f32[512]{0:T(512)} %copy-done.47) | copy-start | bytes 6148
  947.9 4.9 copy-start.23
  952.8 3.4 copy-start.31
  952.8 4.8 copy-start.1
  (25 other events, 45.3 us)
Sparse Core Ops, SparseCore 0:
  9.6 31.2 all-gather.4
  154.7 37.9 reduce-scatter.10
  199.1 28.5 all-gather.6
  246.2 37.9 reduce-scatter.12
  291.6 28.5 all-gather.8
  337.9 37.9 reduce-scatter.14
  382.0 28.5 all-gather.10
  413.2 19.7 reduce-scatter.20
  435.5 19.7 reduce-scatter.18
  604.6 37.9 reduce-scatter.16
  647.7 300.2 all-reduce.3
where the time goes:
time: 971 us; the launch traced here: 964 us
  waiting for transfers between devices  508 us (52%)
  matrix products  219 us (23%)
  local copies, waits for them, and re-layouts  106 us (11%)
  other arithmetic  92.9 us (10%)
  blocking collectives  21.7 us (2%)
  between operations  14.7 us (2%)
    psum x1, waiting for transfers between devices, body(): lax.psum((grad_qkv, grad_out, grad_gate_up, grad_down, norm1_sum, norm2_s...  286 us
    reduce_scatter x1, waiting for transfers between devices, body(): lax.psum_scatter(jnp.dot(attended_flat, w_out, preferred_element_type=jnp...  38.1 us
    reduce_scatter x1, waiting for transfers between devices, body(): lax.psum_scatter(d_normed_part.astype(jnp.bfloat16), 'mp', scatter_dimens...  38.1 us
    reduce_scatter x1, waiting for transfers between devices, body(): lax.psum_scatter(jnp.dot(hidden, w_down, preferred_element_type=jnp.float...  38.1 us
    dynamic_update_slice x8, local copies, waits for them, and re-layouts, attend_back(): lax.scan(step_block, (zero_grad, zero_grad), pieces)  36.1 us
    dot_general x4, matrix products, step_block(): jnp.einsum('qhd,khd->hqk', q_block, keys_all, preferred_element_type=jnp....  35.3 us
    unnamed x119, local copies, waits for them, and re-layouts  34.2 us
    dot_general x4, matrix products, step_block(): jnp.einsum('hqk,qhd->khd', attention.astype(jnp.bfloat16), d_block, prefe...  29.7 us
  transfers between devices with their start and end apart: 11, of which 8 were waited for; matrix products, arithmetic and copies ran while one was open for 24% of the time, Pallas kernels for 0%

commit v1 on v0

v1 whole, which is shorter than its diff:
```python
import functools
import math

import jax
import jax.numpy as jnp
from jax import lax
from jax.experimental import pallas as pl
from jax.experimental.pallas import tpu as pltpu
from jax.sharding import PartitionSpec as P

F32 = jnp.float32
BF16 = jnp.bfloat16
HEAD_DIM = 64
LANES = 128
EPSILON = 1e-05
BLOCK = 256
SEG_COL = 64
SHIFT_COL = 80
FAR = -(2.0**100)
LOG2E = math.log2(math.e)
NT = (((1,), (1,)), ((), ()))
TN = (((0,), (0,)), ((), ()))
NN = (((1,), (0,)), ((), ()))
VMEM_LIMIT = 58 << 20


def mm(a, b, dims=NN):
    return lax.dot_general(a, b, dims, preferred_element_type=F32)


def lane_iota(rows):
    return lax.broadcasted_iota(jnp.int32, (rows, LANES), 1)


def thirds(column):
    high = column.astype(BF16)
    rest = column - high.astype(F32)
    mid = rest.astype(BF16)
    low = (rest - mid.astype(F32)).astype(BF16)
    return high.astype(F32), mid.astype(F32), low.astype(F32)


def shift_columns(column, first, lanes):
    high, mid, low = thirds(column)
    terms = jnp.where(lanes == first, high, 0.0)
    terms = jnp.where(lanes == first + 1, mid, terms)
    return jnp.where(lanes == first + 2, low, terms)


def turn(values, lanes):
    width = values.shape[-1]
    left = pltpu.roll(values, width - 32, 1)
    right = pltpu.roll(values, 32, 1)
    return jnp.where((lanes & 63) < 32, left, right)


def qkv_kernel(place, x_ref, w_ref, cos_ref, sin_ref, bounds_ref, q_ref, k_ref, v_ref):
    rows = x_ref.shape[1]
    heads = q_ref.shape[0]
    width = heads * HEAD_DIM
    shard = place[0] ^ place[1 + pl.program_id(0)]
    tile = BLOCK
    lanes = lane_iota(tile)
    for part in range(rows // tile):
        piece = pl.ds(part * tile, tile)
        projected = mm(x_ref[0, piece, :], w_ref[...])
        cosine, sine = cos_ref[piece, :], sin_ref[piece, :]
        token = lax.broadcasted_iota(jnp.int32, (tile, LANES), 0) + (shard * rows + part * tile)
        inside = (token >= bounds_ref[0:1, :]) & (token < bounds_ref[1:2, :])
        slot = (lanes >= SEG_COL) & (lanes < SHIFT_COL)
        q_tail = jnp.where(slot & ~inside, FAR, 0.0)
        k_tail = jnp.where((slot & inside) | ((lanes >= SHIFT_COL) & (lanes < SHIFT_COL + 3)), 1.0, 0.0)
        v_tail = jnp.where((lanes >= HEAD_DIM) & (lanes < HEAD_DIM + 3), 1.0, 0.0)

        def head_of(column):
            start = column // LANES * LANES
            pair = projected[:, start : min(start + LANES, 3 * width)]
            if pair.shape[1] < LANES:
                pair = jnp.concatenate([pair, pair], axis=1)
            return pair if column % LANES == 0 else pltpu.roll(pair, HEAD_DIM, 1)

        for h in range(heads):
            q = head_of(h * HEAD_DIM)
            q = (q * cosine + turn(q, lanes) * sine) * (LOG2E / math.sqrt(HEAD_DIM))
            q_ref[h, piece, :] = jnp.where(lanes < HEAD_DIM, q, q_tail).astype(BF16)
            k = head_of(width + h * HEAD_DIM)
            k = k * cosine + turn(k, lanes) * sine
            k_ref[h, piece, :] = jnp.where(lanes < HEAD_DIM, k, k_tail).astype(BF16)
            v = head_of(2 * width + h * HEAD_DIM)
            v_ref[h, piece, :] = jnp.where(lanes < HEAD_DIM, v, v_tail).astype(BF16)


def project(x_slots, w_flat, cosine, sine, bounds, place, heads):
    count, rows, width = x_slots.shape
    tokens = count * rows
    out = jax.ShapeDtypeStruct((heads, tokens, LANES), BF16)
    whole = lambda *shape: pl.BlockSpec(shape, lambda s, place: (0,) * len(shape))
    by_shard = pl.BlockSpec((rows, LANES), lambda s, place: (place[0] ^ place[1 + s], 0))
    head_spec = pl.BlockSpec((heads, rows, LANES), lambda s, place: (0, place[0] ^ place[1 + s], 0))
    return pl.pallas_call(
        qkv_kernel,
        out_shape=(out, out, out),
        grid_spec=pltpu.PrefetchScalarGridSpec(
            num_scalar_prefetch=1,
            grid=(count,),
            in_specs=[
                pl.BlockSpec((1, rows, width), lambda s, place: (s, 0, 0)),
                whole(*w_flat.shape),
                by_shard,
                by_shard,
                whole(*bounds.shape),
            ],
            out_specs=[head_spec] * 3,
        ),
        compiler_params=pltpu.CompilerParams(vmem_limit_bytes=VMEM_LIMIT),
        cost_estimate=pl.CostEstimate(
            flops=2 * tokens * width * w_flat.shape[1],
            bytes_accessed=tokens * width * 2 + 3 * heads * tokens * LANES * 2,
            transcendentals=0,
        ),
        name="project",
    )(place, x_slots, w_flat, cosine, sine, bounds)


def attend_kernel(place, ranges, q_ref, k_ref, v_ref, o_ref, qb_ref, top_ref, acc_ref):
    heads = q_ref.shape[0]
    i = pl.program_id(0)
    blocks = pl.num_programs(0)
    first, last = ranges[i], ranges[blocks + i]
    lanes = lane_iota(BLOCK)
    top_ref[...] = jnp.full_like(top_ref, FAR)
    acc_ref[...] = jnp.zeros_like(acc_ref)

    def find_top(j, carry):
        rows = pl.ds(pl.multiple_of(j * BLOCK, BLOCK), BLOCK)
        for h in range(heads):
            s = mm(q_ref[h], k_ref[h, rows, :], NT)
            top_ref[h] = jnp.maximum(top_ref[h], jnp.maximum(s[:, :LANES], s[:, LANES:]))
        return carry

    lax.fori_loop(first, last + 1, find_top, 0)
    tops = []
    for h in range(heads):
        top = jnp.max(top_ref[h], axis=1, keepdims=True)
        tops.append(top)
        qb_ref[h] = q_ref[h] + shift_columns(-top, SHIFT_COL, lanes).astype(BF16)

    def add_up(j, carry):
        rows = pl.ds(pl.multiple_of(j * BLOCK, BLOCK), BLOCK)
        for h in range(heads):
            s = mm(qb_ref[h], k_ref[h, rows, :], NT)
            acc_ref[h] += mm(jnp.exp2(s).astype(BF16), v_ref[h, rows, :])
        return carry

    lax.fori_loop(first, last + 1, add_up, 0)
    for h in range(heads):
        total = acc_ref[h, :, HEAD_DIM : HEAD_DIM + 1]
        o_ref[0, :, h * HEAD_DIM : (h + 1) * HEAD_DIM] = (acc_ref[h, :, :HEAD_DIM] / total).astype(BF16)
        level = tops[h] + jnp.log2(total)
        qb_ref[h] = q_ref[h] + shift_columns(-level, SHIFT_COL, lanes).astype(BF16)


def slot_of(relative):
    return (relative >> 1) | ((relative & 1) << 1)


def attend(q, k, v, place, ranges, shards):
    heads, tokens, _ = q.shape
    blocks = tokens // BLOCK
    rows = tokens // shards
    per = rows // BLOCK
    whole = pl.BlockSpec((heads, tokens, LANES), lambda i, place, ranges: (0, 0, 0))
    mine = pl.BlockSpec((heads, BLOCK, LANES), lambda i, place, ranges: (0, i, 0))
    return pl.pallas_call(
        attend_kernel,
        out_shape=(
            jax.ShapeDtypeStruct((shards, rows, heads * HEAD_DIM), BF16),
            jax.ShapeDtypeStruct((heads, tokens, LANES), BF16),
        ),
        grid_spec=pltpu.PrefetchScalarGridSpec(
            num_scalar_prefetch=2,
            grid=(blocks,),
            in_specs=[mine, whole, whole],
            out_specs=[
                pl.BlockSpec(
                    (1, BLOCK, heads * HEAD_DIM),
                    lambda i, place, ranges: (slot_of((i // per) ^ place[0]), i % per, 0),
                ),
                mine,
            ],
            scratch_shapes=[pltpu.VMEM((heads, BLOCK, LANES), F32), pltpu.VMEM((heads, BLOCK, LANES), F32)],
        ),
        compiler_params=pltpu.CompilerParams(vmem_limit_bytes=VMEM_LIMIT),
        cost_estimate=pl.CostEstimate(
            flops=3 * heads * tokens * tokens * LANES,
            bytes_accessed=5 * heads * tokens * LANES * 2,
            transcendentals=heads * tokens * tokens // 2,
        ),
        name="attend",
    )(place, ranges, q, k, v)


def attend_back_kernel(
    place, ranges, qb_ref, k_ref, v_ref, att_ref, dh_ref, w_ref, cos_ref, sin_ref, out_ref, do_ref, dq_ref, dk_ref, dv_ref
):
    heads, tokens, _ = qb_ref.shape
    shards, rows, _ = att_ref.shape
    blocks = tokens // BLOCK
    per = rows // BLOCK
    width = heads * HEAD_DIM
    lanes = lane_iota(BLOCK)

    def place_of(i):
        return slot_of((i // per) ^ place[0]), pl.ds(pl.multiple_of((i % per) * BLOCK, BLOCK), BLOCK)

    def rows_of(i):
        return pl.ds(pl.multiple_of(i * BLOCK, BLOCK), BLOCK)

    def prepare(i, carry):
        slot, piece = place_of(i)
        d_att = mm(dh_ref[slot, piece, :], w_ref[...], NT)
        for h in range(heads):
            d_head = d_att[:, h * LANES : (h + 1) * LANES].astype(BF16).astype(F32)
            own = att_ref[slot, piece, h * HEAD_DIM : (h + 1) * HEAD_DIM].astype(F32)
            dot = jnp.sum(d_head[:, :HEAD_DIM] * own, axis=1, keepdims=True)
            do_ref[h, rows_of(i), :] = (d_head + shift_columns(-dot, HEAD_DIM, lanes)).astype(BF16)
        return carry

    lax.fori_loop(0, blocks, prepare, 0)
    dq_ref[...] = jnp.zeros_like(dq_ref)

    def rotate_back(values, where):
        return values * cos_ref[where, :] - turn(values, lanes) * sin_ref[where, :]

    def over_keys(j, carry):
        keys = rows_of(j)
        dk_ref[...] = jnp.zeros_like(dk_ref)
        dv_ref[...] = jnp.zeros_like(dv_ref)

        def over_queries(i, carry):
            queries = rows_of(i)
            for h in range(heads):
                k, q, d_out = k_ref[h, keys, :], qb_ref[h, queries, :], do_ref[h, queries, :]
                probs = jnp.exp2(mm(k, q, NT))
                d_scores = (probs * mm(v_ref[h, keys, :], d_out, NT)).astype(BF16)
                dv_ref[h] += mm(probs.astype(BF16), d_out)
                dk_ref[h] += mm(d_scores, q)
                dq_ref[h, queries, :] += mm(d_scores, k, TN)
            return carry

        lax.fori_loop(ranges[j], ranges[blocks + j] + 1, over_queries, 0)
        slot, piece = place_of(j)
        for h in range(heads):
            d_key = rotate_back(dk_ref[h] * (1.0 / LOG2E), keys)
            column = width + h * HEAD_DIM
            out_ref[slot, piece, column : column + HEAD_DIM] = d_key[:, :HEAD_DIM].astype(BF16)
            column = 2 * width + h * HEAD_DIM
            out_ref[slot, piece, column : column + HEAD_DIM] = dv_ref[h, :, :HEAD_DIM].astype(BF16)
        return carry

    lax.fori_loop(0, blocks, over_keys, 0)

    def finish(i, carry):
        slot, piece = place_of(i)
        for h in range(heads):
            d_query = rotate_back(dq_ref[h, rows_of(i), :] * (1.0 / math.sqrt(HEAD_DIM)), rows_of(i))
            out_ref[slot, piece, h * HEAD_DIM : (h + 1) * HEAD_DIM] = d_query[:, :HEAD_DIM].astype(BF16)
        return carry

    lax.fori_loop(0, blocks, finish, 0)


def attend_back(qb, k, v, att, dh_slots, w_out, cosine, sine, place, ranges):
    heads, tokens, _ = qb.shape
    shards, rows, _ = att.shape
    w_wide = jnp.pad(w_out.reshape(heads, HEAD_DIM, -1), ((0, 0), (0, LANES - HEAD_DIM), (0, 0)))
    w_wide = w_wide.reshape(heads * LANES, -1)
    vmem = pl.BlockSpec(memory_space=pltpu.VMEM)
    smem = pl.BlockSpec(memory_space=pltpu.SMEM)
    return pl.pallas_call(
        attend_back_kernel,
        out_shape=jax.ShapeDtypeStruct((shards, rows, 3 * heads * HEAD_DIM), BF16),
        in_specs=[smem, smem] + [vmem] * 8,
        out_specs=vmem,
        scratch_shapes=[
            pltpu.VMEM((heads, tokens, LANES), BF16),
            pltpu.VMEM((heads, tokens, LANES), F32),
            pltpu.VMEM((heads, BLOCK, LANES), F32),
            pltpu.VMEM((heads, BLOCK, LANES), F32),
        ],
        compiler_params=pltpu.CompilerParams(vmem_limit_bytes=VMEM_LIMIT),
        cost_estimate=pl.CostEstimate(
            flops=5 * heads * tokens * tokens * LANES,
            bytes_accessed=6 * heads * tokens * LANES * 2,
            transcendentals=heads * tokens * tokens // 2,
        ),
        name="attend_back",
    )(place, ranges, qb, k, v, att, dh_slots, w_wide, cosine, sine)


def doc_tables(lengths, tokens, blocks):
    ends = jnp.cumsum(lengths)
    starts = ends - lengths
    places = jnp.arange(tokens, dtype=jnp.int32)
    inside = (places[:, None] >= starts[None, :]) & (places[:, None] < ends[None, :])
    positions = places - jnp.sum(jnp.where(inside, starts[None, :], 0), axis=1)
    edge = jnp.arange(blocks, dtype=jnp.int32) * BLOCK
    touches = (starts[None, :] < edge[:, None] + BLOCK) & (ends[None, :] > edge[:, None])
    first = jnp.min(jnp.where(touches, starts[None, :], tokens), axis=1) // BLOCK
    last = (jnp.max(jnp.where(touches, ends[None, :], 0), axis=1) - 1) // BLOCK
    ranges = jnp.concatenate([first, last]).astype(jnp.int32)
    pad = (SEG_COL, LANES - SEG_COL - lengths.shape[0])
    bounds = jnp.stack([jnp.pad(starts, pad), jnp.pad(ends, pad)]).astype(jnp.int32)
    return positions, ranges, jnp.pad(bounds, ((0, 6), (0, 0)))


def rotary(positions):
    lane = jnp.arange(LANES, dtype=jnp.int32)
    rate = jnp.exp((lane & 31).astype(F32) * (-2.0 * math.log(1000.0) / HEAD_DIM))
    angles = positions.astype(F32)[:, None] * rate[None, :]
    sign = jnp.where((lane & 63) < 32, -1.0, 1.0)
    return jnp.cos(angles), jnp.sin(angles) * sign[None, :]


def reduce_over_dp(total, bits, me):
    size = lax.axis_size("dp")

    def exchange(values, bit):
        return lax.ppermute(values, "dp", [(i, i ^ (1 << bit)) for i in range(size)])

    for bit in bits:
        half = total.shape[0] // 2
        mine = (me >> bit) & 1
        give = lax.dynamic_slice_in_dim(total, (1 - mine) * half, half, 0).astype(BF16)
        keep = lax.dynamic_slice_in_dim(total, mine * half, half, 0)
        total = keep + exchange(give, bit).astype(F32)
    total = total.astype(BF16)
    for bit in reversed(bits):
        mine = (me >> bit) & 1
        other = exchange(total, bit)
        total = jnp.where(mine == 0, jnp.concatenate([total, other]), jnp.concatenate([other, total]))
    return total


def body(
    tokens, lengths, w_qkv, w_out, w_gate_up, w_down, ln1_scale, ln1_shift, ln2_scale, ln2_shift, cotangent
):
    rows, width = tokens.shape
    shards = lax.axis_size("mp")
    length = rows * shards
    local_cols = w_out.shape[0]
    heads = local_cols // HEAD_DIM
    hidden_cols = w_down.shape[0]
    m = lax.axis_index("mp")
    dp_bits = list(range(int(math.log2(lax.axis_size("dp")))))
    me = lax.axis_index("dp")

    def swap(values, distance):
        return lax.ppermute(values, "mp", [(i, i ^ distance) for i in range(shards)])

    across = lambda values: swap(values, 2)
    beside = lambda values: swap(values, 1)

    x_far = across(tokens)
    x_near = beside(tokens)
    x_last = beside(x_far)
    positions, ranges, bounds = doc_tables(lengths[0], length, length // BLOCK)
    cosine, sine = rotary(positions)
    place = jnp.stack([m.astype(jnp.int32)] + [jnp.int32(r) for r in (0, 2, 1, 3)])
    flat_qkv = w_qkv.reshape(width, 3 * local_cols)
    w_qkv_near = beside(flat_qkv)
    w_out_near = beside(w_out)
    flat_gate_up = w_gate_up.reshape(width, 2 * hidden_cols)
    w_gate_up_near = beside(flat_gate_up)
    w_down_near = beside(w_down)
    x_slots = jnp.stack([tokens, x_far, x_near, x_last])
    q, k, v = project(x_slots, flat_qkv, cosine, sine, bounds, place, heads)
    att, qb = attend(q, k, v, place, ranges, shards)
    att_near = beside(att[2:])

    def out_project(index):
        return mm(att[index], w_out) + mm(att_near[index], w_out_near)

    branch_far = across(out_project(1).astype(BF16))
    h = tokens.astype(F32) + out_project(0) + branch_far.astype(F32)
    h = h - jnp.mean(h, axis=-1, keepdims=True)
    r1 = lax.rsqrt(jnp.mean(h * h, axis=-1, keepdims=True) + EPSILON)
    h_hat = h * r1
    normed = h_hat * ln1_scale + ln1_shift
    normed_low = normed.astype(BF16)
    normed_far = across(normed_low)

    w_ins, w_downs = (flat_gate_up, w_gate_up_near), (w_down, w_down_near)

    def mlp(values):
        kept, partial = [], 0.0
        for w_in, w_back in zip(w_ins, w_downs):
            gate_up = mm(values, w_in)
            gate, up = gate_up[:, :hidden_cols], gate_up[:, hidden_cols:]
            hidden = (gate * jax.nn.sigmoid(gate) * up).astype(BF16)
            partial = partial + mm(hidden, w_back)
            kept.append((gate_up.astype(BF16), hidden))
        return partial, kept

    partial_own, kept_own = mlp(normed_low)
    partial_far, kept_far = mlp(normed_far)
    mlp_far = across(partial_far.astype(BF16))
    z = normed + partial_own + mlp_far.astype(F32)
    z = z - jnp.mean(z, axis=-1, keepdims=True)
    r2 = lax.rsqrt(jnp.mean(z * z, axis=-1, keepdims=True) + EPSILON)
    z_hat = z * r2
    output = (z_hat * ln2_scale + ln2_shift).astype(BF16)
    g = cotangent.astype(F32)
    e = g * ln2_scale
    dz = r2 * (e - jnp.mean(e, axis=-1, keepdims=True) - z_hat * jnp.mean(e * z_hat, axis=-1, keepdims=True))
    d_scale_two, d_shift_two = jnp.sum(g * z_hat, axis=0), jnp.sum(g, axis=0)
    dz_low = dz.astype(BF16)
    dz_far = across(dz_low)

    def mlp_back(d_out, kept):
        d_normed, d_ins = 0.0, []
        for (gate_up, hidden), w_in, w_back in zip(kept, w_ins, w_downs):
            gate, up = gate_up[:, :hidden_cols].astype(F32), gate_up[:, hidden_cols:].astype(F32)
            d_hidden = mm(d_out, w_back, NT)
            s = jax.nn.sigmoid(gate)
            d_gate = (d_hidden * up * s * (1.0 + gate * (1.0 - s))).astype(BF16)
            d_up = (d_hidden * gate * s).astype(BF16)
            d_in = jnp.concatenate([d_gate, d_up], axis=1)
            d_normed = d_normed + mm(d_in, w_in, NT)
            d_ins.append(d_in)
        return d_normed, d_ins

    d_own, d_ins_own = mlp_back(dz_low, kept_own)
    d_far, d_ins_far = mlp_back(dz_far, kept_far)
    d_normed_far = across(d_far.astype(BF16))

    def weight_grads(core):
        down = mm(kept_own[core][1], dz_low, TN) + mm(kept_far[core][1], dz_far, TN)
        gate_up = mm(normed_low, d_ins_own[core], TN) + mm(normed_far, d_ins_far[core], TN)
        return gate_up, down

    grad_gate_up, grad_down = weight_grads(1)
    grad_gate_up_near, grad_down_near = beside(grad_gate_up.astype(BF16)), beside(grad_down.astype(BF16))
    grad_gate_up, grad_down = weight_grads(0)
    grad_gate_up = grad_gate_up + grad_gate_up_near.astype(F32)
    grad_down = grad_down + grad_down_near.astype(F32)
    swapped = [dp_bits[1], dp_bits[0]] + dp_bits[2:] if len(dp_bits) > 1 else dp_bits
    half = width // 2
    grad_gate_up = jnp.concatenate(
        [reduce_over_dp(grad_gate_up[:half], dp_bits, me), reduce_over_dp(grad_gate_up[half:], swapped, me)]
    ).astype(F32)
    grad_down = jnp.concatenate(
        [
            reduce_over_dp(grad_down[: hidden_cols // 2], dp_bits, me),
            reduce_over_dp(grad_down[hidden_cols // 2 :], swapped, me),
        ]
    ).astype(F32)

    d_normed = dz + d_own + d_normed_far.astype(F32)
    e1 = d_normed * ln1_scale
    dh = r1 * (e1 - jnp.mean(e1, axis=-1, keepdims=True) - h_hat * jnp.mean(e1 * h_hat, axis=-1, keepdims=True))
    d_scale_one, d_shift_one = jnp.sum(d_normed * h_hat, axis=0), jnp.sum(d_normed, axis=0)
    dh_low = dh.astype(BF16)
    dh_far = across(dh_low)
    dh_near = beside(dh_low)
    dh_last = beside(dh_far)
    dh_slots = jnp.stack([dh_low, dh_far, dh_near, dh_last])
    d_qkv = attend_back(qb, k, v, att, dh_slots, w_out, cosine, sine, place, ranges)
    grad_out = mm(att.reshape(length, local_cols), dh_slots.reshape(length, width), TN)
    d_qkv_near = beside(d_qkv[2:])
    d_x_far = mm(d_qkv[1], flat_qkv, NT) + mm(d_qkv_near[1], w_qkv_near, NT)
    d_x_far = across(d_x_far.astype(BF16))
    d_x_own = mm(d_qkv[0], flat_qkv, NT) + mm(d_qkv_near[0], w_qkv_near, NT)
    grad_qkv = mm(x_slots.reshape(length, width), d_qkv.reshape(length, 3 * local_cols), TN)
    d_tokens = (dh + d_x_own + d_x_far.astype(F32)).astype(BF16)
    grad_qkv = jnp.concatenate(
        [reduce_over_dp(grad_qkv[:half], dp_bits, me), reduce_over_dp(grad_qkv[half:], swapped, me)]
    ).astype(F32)
    grad_out = reduce_over_dp(grad_out, swapped, me).astype(F32)
    norms = lax.psum(jnp.stack([d_scale_one, d_shift_one, d_scale_two, d_shift_two]), ("dp", "mp"))
    norms = lax.dynamic_slice_in_dim(norms, m * local_cols, local_cols, 1)
    return (
        output,
        d_tokens,
        grad_qkv.reshape(width, 3, local_cols),
        grad_out,
        grad_gate_up.reshape(width, 2, hidden_cols),
        grad_down,
        norms[0],
        norms[1],
        norms[2],
        norms[3],
    )


def solution(mesh):
    return jax.shard_map(
        body,
        mesh=mesh,
        in_specs=(
            P(("dp", "mp"), None),
            P("dp", None),
            P(None, None, "mp"),
            P("mp", None),
            P(None, None, "mp"),
            P("mp", None),
            P(),
            P(),
            P(),
            P(),
            P(("dp", "mp"), None),
        ),
        out_specs=(
            P(("dp", "mp"), None),
            P(("dp", "mp"), None),
            P(None, None, "mp"),
            P("mp", None),
            P(None, None, "mp"),
            P("mp", None),
            P("mp"),
            P("mp"),
            P("mp"),
            P("mp"),
        ),
        check_vma=False,
    )
```

time: 971 us -> 542 us (0.56)
  waiting for transfers between devices: 508 us -> 166 us
  matrix products: 219 us -> 69.9 us
  Pallas kernels: 0 us -> 104 us
  local copies, waits for them, and re-layouts: 106 us -> 23.2 us
  starting transfers between devices: 1.24 us -> 67.2 us
  other arithmetic: 92.9 us -> 63.4 us
  blocking collectives: 21.7 us -> 40.2 us
  between operations: 14.7 us -> 1.94 us
    psum x1 -> x0, waiting for transfers between devices: 286 us -> none  [body(): lax.psum((grad_qkv, grad_out, grad_gate_up, grad_down, norm1_sum, norm2_s...]
    ppermute x0 -> x62, waiting for transfers between devices: none -> 166 us  [the longest x42 103 us: exchange(): return lax.ppermute(values, 'dp', [(i, i ^ 1 << bit) for i in range(size)])]
    dot_general x40 -> x34, matrix products: 219 us -> 69.9 us  [mm(): return lax.dot_general(a, b, dims, preferred_element_type=F32)]
    reduce_scatter x4 -> x0, waiting for transfers between devices: 114 us -> none  [the longest x1 38.1 us: body(): lax.psum_scatter(jnp.dot(attended_flat, w_out, preferred_element_type=jnp...]
    all_gather x4 -> x0, waiting for transfers between devices: 107 us -> none  [the longest x1 28.3 us: body(): lax.all_gather(d_sum.astype(jnp.bfloat16), 'mp', axis=0, tiled=True)]
    pallas_call x0 -> x3, Pallas kernels: none -> 104 us  [the longest x1 54.6 us: attend_back(): pl.pallas_call(attend_back_kernel, out_shape=jax.ShapeDtypeStruct((shards...]
    ppermute x0 -> x62, starting transfers between devices: none -> 67.2 us  [the longest x42 51.3 us: exchange(): return lax.ppermute(values, 'dp', [(i, i ^ 1 << bit) for i in range(size)])]
    dynamic_update_slice x8 -> x0, local copies, waits for them, and re-layouts: 36.1 us -> none  [attend_back(): lax.scan(step_block, (zero_grad, zero_grad), pieces)]
  transfers between devices with their start and end apart: 11 -> 62, of which waited for: 8 -> 33; matrix products, arithmetic and copies ran while one was open for 24% -> 26% of each run, Pallas kernels for 0% -> 10%
where the time goes in v1:
time: 542 us; the launch traced here: 536 us
  waiting for transfers between devices  166 us (31%)
  Pallas kernels  104 us (19%)
  matrix products  69.9 us (13%)
  starting transfers between devices  67.2 us (12%)
  other arithmetic  63.4 us (12%)
  blocking collectives  40.2 us (7%)
  local copies, waits for them, and re-layouts  23.2 us (4%)
    ppermute x42, waiting for transfers between devices, exchange(): return lax.ppermute(values, 'dp', [(i, i ^ 1 << bit) for i in range(size)])  103 us
    dot_general x34, matrix products, mm(): return lax.dot_general(a, b, dims, preferred_element_type=F32)  69.9 us
    ppermute x20, waiting for transfers between devices, swap(): lax.ppermute(values, 'mp', [(i, i ^ distance) for i in range(shards)])  63 us
    pallas_call x1, Pallas kernels, attend_back(): pl.pallas_call(attend_back_kernel, out_shape=jax.ShapeDtypeStruct((shards...  54.6 us
    ppermute x42, starting transfers between devices, exchange(): return lax.ppermute(values, 'dp', [(i, i ^ 1 << bit) for i in range(size)])  51.3 us
    psum x1, blocking collectives, body(): lax.psum(jnp.stack([d_scale_one, d_shift_one, d_scale_two, d_shift_two]),...  40.2 us
    pallas_call x1, Pallas kernels, attend(): pl.pallas_call(attend_kernel, out_shape=(jax.ShapeDtypeStruct((shards, ro...  39.3 us
    select_n x28, other arithmetic, reduce_over_dp(): jnp.where(mine == 0, jnp.concatenate([total, other]), jnp.concatenate([ot...  25.9 us
  transfers between devices with their start and end apart: 62, of which 33 were waited for; matrix products, arithmetic and copies ran while one was open for 26% of the time, Pallas kernels for 10%

profile of v1, /device:TPU:0, one launch (start us, length us, event | category | flops | bytes accessed | tf_op | source)
XLA Modules:
  0.0 536.3 jit_solution(17629248626052797503)
XLA Ops:
  0.7 3.0 collective-permute-start
  8.6 12.8 %collective-permute-done = bf16[512,768]{1,0:T(8,128)(2,1)S(1)} collective-permute-done((bf16[512,768]{1,0:T(8,128)(2,1)}, bf16[512,768]{1,0:T(8,128)(2,1)S(1)}, u32[]{:S(2)}, u32[]{:S(2)}) %collective-permute-start) | collective-permute-done | bytes 786464 | tf_op jit(solution)/shard_map/ppermute | solution.py:359
  22.2 5.6 %fusion.44 = (f32[2048,128]{1,0:T(8,128)}, f32[2048,128]{1,0:T(8,128)}) fusion(f32[128]{0:T(128)S(1)} %get-tuple-element.70, f32[128]{0:T(128)S(1)} %get-tuple-element.71, f32[2048]{0:T(1024)S(1)} %subtract_convert_fusion), kind=kLoop, calls=%fused_computation.105 | loop fusion | flops 524288 | bytes 2106368 | tf_op jit(solution)/shard_map/mul | solution.py:322
  29.9 10.3 %project.1 = (bf16[3,2048,128]{2,1,0:T(8,128)(2,1)}, bf16[3,2048,128]{2,1,0:T(8,128)(2,1)}, bf16[3,2048,128]{2,1,0:T(8,128)(2,1)}) custom-call(s32[5]{0:T(128)} %stack.61.place, bf16[4,512,768]{2,1,0:T(8,128)(2,1)} %pad_maximum_fusion.x_ref, bf16[768,576]{1,0:T(8,128)(2,1)} %copy.35.w_ref, f32[2048,128]{1,0:T(8,128)} %get-tuple-element.57.cos_ref, ...), custom_call_target="tpu_custom_call" | custom-call | flops 1811939328 | bytes 7864320 | tf_op jit(solution)/shard_map/project/pallas_call | solution.py:100
  40.2 39.3 %attend.1 = (bf16[4,512,192]{2,1,0:T(8,128)(2,1)}, bf16[3,2048,128]{2,1,0:T(8,128)(2,1)}) custom-call(s32[5]{0:T(128)} %stack.61.place, s32[16]{0:T(128)} %pad_add_fusion.1.ranges, bf16[3,2048,128]{2,1,0:T(8,128)(2,1)} %get-tuple-element.15.q_ref, bf16[3,2048,128]{2,1,0:T(8,128)(2,1)} %get-tuple-element.16.k_ref, bf16[3,2048,128]{2,1,0:T(8,128)(2,1)} %get-tuple-element.17.v_ref), custom_call_target="tpu_custom_call" | custom-call | flops 4831838208 | bytes 7864320 | tf_op jit(solution)/shard_map/attend/pallas_call | solution.py:174
  89.8 14.6 %collective-permute-done.5 = bf16[512,768]{1,0:T(8,128)(2,1)} collective-permute-done((bf16[512,768]{1,0:T(8,128)(2,1)}, bf16[512,768]{1,0:T(8,128)(2,1)}, u32[]{:S(2)}, u32[]{:S(2)}) %collective-permute-start.5) | collective-permute-done | bytes 786464 | tf_op jit(solution)/shard_map/ppermute | solution.py:359
  110.7 3.0 fusion.83
  113.7 12.3 %collective-permute-done.8 = bf16[512,768]{1,0:T(8,128)(2,1)S(1)} collective-permute-done((bf16[512,768]{1,0:T(8,128)(2,1)S(1)}, bf16[512,768]{1,0:T(8,128)(2,1)S(1)}, u32[]{:S(2)}, u32[]{:S(2)}) %collective-permute-start.8) | collective-permute-done | bytes 786464 | tf_op jit(solution)/shard_map/ppermute | solution.py:359
  130.0 3.0 fusion.81
  142.0 11.8 %collective-permute-done.9 = bf16[512,768]{1,0:T(8,128)(2,1)S(1)} collective-permute-done((bf16[512,768]{1,0:T(8,128)(2,1)S(1)}, bf16[512,768]{1,0:T(8,128)(2,1)S(1)}, u32[]{:S(2)}, u32[]{:S(2)}) %collective-permute-start.9) | collective-permute-done | bytes 786464 | tf_op jit(solution)/shard_map/ppermute | solution.py:359
  166.4 3.6 fusion.49
  172.2 3.1 fusion.48
  181.6 3.1 add_convert_fusion.4
  186.9 3.0 add_convert_fusion
  190.7 11.0 %collective-permute-done.11 = bf16[512,768]{1,0:T(8,128)(2,1)S(1)} collective-permute-done((bf16[512,768]{1,0:T(8,128)(2,1)S(1)}, bf16[512,768]{1,0:T(8,128)(2,1)S(1)}, u32[]{:S(2)}, u32[]{:S(2)}) %collective-permute-start.11) | collective-permute-done | bytes 786464 | tf_op jit(solution)/shard_map/ppermute | solution.py:359
  216.8 2.6 collective-permute-start.58
  219.3 2.6 collective-permute-done.51
  225.4 2.7 collective-permute-done.52
  233.8 3.6 fusion.45
  241.8 40.2 %psum.7 = f32[4,768]{1,0:T(4,128)S(1)} all-reduce(f32[4,768]{1,0:T(4,128)S(1)} %pad_maximum_fusion.14), channel_id=1, replica_groups=mesh['dp'=8,'mp'=4] {'dp','mp'}, use_global_device_ids=true, to_apply=%region_16.17 | all-reduce | flops 3072 | bytes 24576 | tf_op jit(solution)/shard_map/psum | solution.py:480
  285.7 3.0 pad_maximum_fusion.1.dh_ref
  288.7 54.6 %attend_back.1 = bf16[4,512,576]{2,1,0:T(8,128)(2,1)} custom-call(s32[5]{0:T(128)} %stack.61.place, s32[16]{0:T(128)} %pad_add_fusion.1.ranges, bf16[3,2048,128]{2,1,0:T(8,128)(2,1)} %get-tuple-element.19.qb_ref, bf16[3,2048,128]{2,1,0:T(8,128)(2,1)} %get-tuple-element.16.k_ref, bf16[3,2048,128]{2,1,0:T(8,128)(2,1)} %get-tuple-element.17.v_ref, ...), custom_call_target="tpu_custom_call" | custom-call | flops 8053063680 | bytes 9437184 | tf_op jit(solution)/shard_map/attend_back/pallas_call | solution.py:280
  346.8 4.8 convolution_bitcast_fusion
  358.4 3.1 convert_add_fusion
  372.4 8.4 %collective-permute-done.32 = bf16[24,768]{1,0:T(8,128)(2,1)S(1)} collective-permute-done((bf16[24,768]{1,0:T(8,128)(2,1)S(1)}, bf16[24,768]{1,0:T(8,128)(2,1)S(1)}, u32[]{:S(2)}, u32[]{:S(2)}) %collective-permute-start.32) | collective-permute-done | bytes 36896 | tf_op jit(solution)/shard_map/ppermute | solution.py:329
  380.8 3.4 collective-permute-start.33
  388.0 3.4 collective-permute-done.25
  393.9 2.8 collective-permute-done.19
  401.1 2.7 collective-permute-start.26
  403.8 6.5 %collective-permute-done.26 = bf16[48,576]{0,1:T(8,128)(2,1)S(1)} collective-permute-done((bf16[48,576]{0,1:T(8,128)(2,1)S(1)}, bf16[48,576]{0,1:T(8,128)(2,1)S(1)}, u32[]{:S(2)}, u32[]{:S(2)}) %collective-permute-start.26) | collective-permute-done | bytes 55328 | tf_op jit(solution)/shard_map/ppermute | solution.py:329
  410.5 9.2 %collective-permute-done.20 = bf16[48,576]{0,1:T(8,128)(2,1)S(1)} collective-permute-done((bf16[48,576]{0,1:T(8,128)(2,1)S(1)}, bf16[48,576]{0,1:T(8,128)(2,1)S(1)}, u32[]{:S(2)}, u32[]{:S(2)}) %collective-permute-start.20) | collective-permute-done | bytes 55328 | tf_op jit(solution)/shard_map/ppermute | solution.py:329
  419.8 8.7 %collective-permute-done.27 = bf16[48,576]{0,1:T(8,128)(2,1)S(1)} collective-permute-done((bf16[48,576]{0,1:T(8,128)(2,1)S(1)}, bf16[48,576]{0,1:T(8,128)(2,1)S(1)}, u32[]{:S(2)}, u32[]{:S(2)}) %collective-permute-start.27) | collective-permute-done | bytes 55328 | tf_op jit(solution)/shard_map/ppermute | solution.py:329
  428.7 7.0 %collective-permute-done.21 = bf16[48,576]{0,1:T(8,128)(2,1)S(1)} collective-permute-done((bf16[48,576]{0,1:T(8,128)(2,1)S(1)}, bf16[48,576]{0,1:T(8,128)(2,1)S(1)}, u32[]{:S(2)}, u32[]{:S(2)}) %collective-permute-start.21) | collective-permute-done | bytes 55328 | tf_op jit(solution)/shard_map/ppermute | solution.py:329
  436.2 6.0 %collective-permute-done.35 = bf16[96,768]{1,0:T(8,128)(2,1)S(1)} collective-permute-done((bf16[96,768]{1,0:T(8,128)(2,1)S(1)}, bf16[96,768]{1,0:T(8,128)(2,1)S(1)}, u32[]{:S(2)}, u32[]{:S(2)}) %collective-permute-start.35) | collective-permute-done | bytes 147488 | tf_op jit(solution)/shard_map/ppermute | solution.py:329
  444.7 4.2 collective-permute-done.28
  449.5 6.0 %collective-permute-done.22 = bf16[96,576]{0,1:T(8,128)(2,1)S(1)} collective-permute-done((bf16[96,576]{0,1:T(8,128)(2,1)S(1)}, bf16[96,576]{0,1:T(8,128)(2,1)S(1)}, u32[]{:S(2)}, u32[]{:S(2)}) %collective-permute-start.22) | collective-permute-done | bytes 110624 | tf_op jit(solution)/shard_map/ppermute | solution.py:329
  458.8 6.3 %collective-permute-done.29 = bf16[192,576]{0,1:T(8,128)(2,1)S(1)} collective-permute-done((bf16[192,576]{0,1:T(8,128)(2,1)S(1)}, bf16[192,576]{0,1:T(8,128)(2,1)S(1)}, u32[]{:S(2)}, u32[]{:S(2)}) %collective-permute-start.29) | collective-permute-done | bytes 221216 | tf_op jit(solution)/shard_map/ppermute | solution.py:329
  467.8 2.7 collective-permute-start.45
  470.4 4.4 collective-permute-done.38
  478.1 5.7 %collective-permute-done.39 = bf16[48,1536]{1,0:T(8,128)(2,1)S(1)} collective-permute-done((bf16[48,1536]{1,0:T(8,128)(2,1)S(1)}, bf16[48,1536]{1,0:T(8,128)(2,1)S(1)}, u32[]{:S(2)}, u32[]{:S(2)}) %collective-permute-start.39) | collective-permute-done | bytes 147488 | tf_op jit(solution)/shard_map/ppermute | solution.py:329
  485.6 3.0 add_convert_fusion.3
  502.9 2.5 broadcast_select_fusion.5
  511.6 3.3 broadcast_select_fusion.2
  517.2 3.1 add_convert_fusion.2
  520.3 2.7 concatenate.305
  523.0 3.7 broadcast_select_fusion
  528.7 2.8 broadcast_select_fusion.1
  531.5 4.6 maximum_convert_fusion
  (317 shorter events, 164.4 us)
Async XLA Ops:
  0.7 20.8 %collective-permute-start = (bf16[512,768]{1,0:T(8,128)(2,1)}, bf16[512,768]{1,0:T(8,128)(2,1)S(1)}, u32[]{:S(2)}, u32[]{:S(2)}) collective-permute-start(bf16[512,768]{1,0:T(8,128)(2,1)} %param.11), channel_id=1, source_target_pairs={{0,2},{1,3},{2,0},{3,1},{4,6},{5,7},{6,4},{7,5},{8,10},{9,11},{10,... | collective-permute-start | bytes 2359304 | tf_op jit(solution)/shard_map/ppermute | solution.py:359
  3.7 24.1 %collective-permute-start.1 = (bf16[512,768]{1,0:T(8,128)(2,1)}, bf16[512,768]{1,0:T(8,128)(2,1)S(1)}, u32[]{:S(2)}, u32[]{:S(2)}) collective-permute-start(bf16[512,768]{1,0:T(8,128)(2,1)} %param.11), channel_id=1, source_target_pairs={{0,1},{1,0},{2,3},{3,2},{4,5},{5,4},{6,7},{7,6},{8,9},{9,8},{10,11... | collective-permute-start | bytes 2359304 | tf_op jit(solution)/shard_map/ppermute | solution.py:359
  84.3 20.1 %collective-permute-start.5 = (bf16[512,768]{1,0:T(8,128)(2,1)}, bf16[512,768]{1,0:T(8,128)(2,1)}, u32[]{:S(2)}, u32[]{:S(2)}) collective-permute-start(bf16[512,768]{1,0:T(8,128)(2,1)} %add_convert_fusion.7), channel_id=1, source_target_pairs={{0,2},{1,3},{2,0},{3,1},{4,6},{5,7},{6,4},{7,5},{8,10},{9,11},{10,... | collective-permute-start | bytes 2359304 | tf_op jit(solution)/shard_map/ppermute | solution.py:359
  86.0 399.6 %collective-permute-start.16 = (bf16[768,576]{0,1:T(8,128)(2,1)S(1)}, bf16[768,576]{0,1:T(8,128)(2,1)}, u32[]{:S(2)}, u32[]{:S(2)}) collective-permute-start(bf16[768,576]{0,1:T(8,128)(2,1)S(1)} %bitcast.130), channel_id=1, source_target_pairs={{0,1},{1,0},{2,3},{3,2},{4,5},{5,4},{6,7},{7,6},{8,9},{9,8},{10,11... | collective-permute-start | bytes 2654216 | tf_op jit(solution)/shard_map/ppermute | solution.py:359
  86.6 24.1 %collective-permute-start.6 = (bf16[768,1536]{1,0:T(8,128)(2,1)S(1)}, bf16[768,1536]{1,0:T(8,128)(2,1)}, u32[]{:S(2)}, u32[]{:S(2)}) collective-permute-start(bf16[768,1536]{1,0:T(8,128)(2,1)S(1)} %bitcast.120), channel_id=1, source_target_pairs={{0,1},{1,0},{2,3},{3,2},{4,5},{5,4},{6,7},{7,6},{8,9},{9,8},{10,11... | collective-permute-start | bytes 7077896 | tf_op jit(solution)/shard_map/ppermute | solution.py:359
  87.1 46.5 %collective-permute-start.7 = (bf16[768,768]{1,0:T(8,128)(2,1)}, bf16[768,768]{1,0:T(8,128)(2,1)}, u32[]{:S(2)}, u32[]{:S(2)}) collective-permute-start(bf16[768,768]{1,0:T(8,128)(2,1)} %param.16), channel_id=1, source_target_pairs={{0,1},{1,0},{2,3},{3,2},{4,5},{5,4},{6,7},{7,6},{8,9},{9,8},{10,11... | collective-permute-start | bytes 3538952 | tf_op jit(solution)/shard_map/ppermute | solution.py:359
  107.0 19.1 %collective-permute-start.8 = (bf16[512,768]{1,0:T(8,128)(2,1)S(1)}, bf16[512,768]{1,0:T(8,128)(2,1)S(1)}, u32[]{:S(2)}, u32[]{:S(2)}) collective-permute-start(bf16[512,768]{1,0:T(8,128)(2,1)S(1)} %fusion.43), channel_id=1, source_target_pairs={{0,2},{1,3},{2,0},{3,1},{4,6},{5,7},{6,4},{7,5},{8,10},{9,11},{10,... | collective-permute-start | bytes 2359304 | tf_op jit(solution)/shard_map/ppermute | solution.py:359
  135.6 18.2 %collective-permute-start.9 = (bf16[512,768]{1,0:T(8,128)(2,1)S(1)}, bf16[512,768]{1,0:T(8,128)(2,1)S(1)}, u32[]{:S(2)}, u32[]{:S(2)}) collective-permute-start(bf16[512,768]{1,0:T(8,128)(2,1)S(1)} %add_convert_fusion.6), channel_id=1, source_target_pairs={{0,2},{1,3},{2,0},{3,1},{4,6},{5,7},{6,4},{7,5},{8,10},{9,11},{10,... | collective-permute-start | bytes 2359304 | tf_op jit(solution)/shard_map/ppermute | solution.py:359
  157.4 17.9 %collective-permute-start.10 = (bf16[512,768]{1,0:T(8,128)(2,1)S(1)}, bf16[512,768]{1,0:T(8,128)(2,1)S(1)}, u32[]{:S(2)}, u32[]{:S(2)}) collective-permute-start(bf16[512,768]{1,0:T(8,128)(2,1)S(1)} %fusion.72), channel_id=1, source_target_pairs={{0,2},{1,3},{2,0},{3,1},{4,6},{5,7},{6,4},{7,5},{8,10},{9,11},{10,... | collective-permute-start | bytes 2359304 | tf_op jit(solution)/shard_map/ppermute | solution.py:359
  184.7 17.0 %collective-permute-start.11 = (bf16[512,768]{1,0:T(8,128)(2,1)S(1)}, bf16[512,768]{1,0:T(8,128)(2,1)S(1)}, u32[]{:S(2)}, u32[]{:S(2)}) collective-permute-start(bf16[512,768]{1,0:T(8,128)(2,1)S(1)} %add_convert_fusion.4), channel_id=1, source_target_pairs={{0,2},{1,3},{2,0},{3,1},{4,6},{5,7},{6,4},{7,5},{8,10},{9,11},{10,... | collective-permute-start | bytes 2359304 | tf_op jit(solution)/shard_map/ppermute | solution.py:359
  186.8 17.1 %collective-permute-start.49 = (bf16[768,768]{1,0:T(8,128)(2,1)S(1)}, bf16[768,768]{1,0:T(8,128)(2,1)S(1)}, u32[]{:S(2)}, u32[]{:S(2)}) collective-permute-start(bf16[768,768]{1,0:T(8,128)(2,1)S(1)} %add_convert_fusion.1), channel_id=1, source_target_pairs={{0,1},{1,0},{2,3},{3,2},{4,5},{5,4},{6,7},{7,6},{8,9},{9,8},{10,11... | collective-permute-start | bytes 3538952 | tf_op jit(solution)/shard_map/ppermute | solution.py:359
  204.5 6.8 %collective-permute-start.56 = (bf16[192,768]{1,0:T(8,128)(2,1)S(1)}, bf16[192,768]{1,0:T(8,128)(2,1)S(1)}, u32[]{:S(2)}, u32[]{:S(2)}) collective-permute-start(bf16[192,768]{1,0:T(8,128)(2,1)S(1)} %dynamic-slice_convert_fusion.2), channel_id=1, source_target_pairs={{0,8},{4,12},{8,0},{12,4},{16,24},{20,28},{24,16},{28,20},{1,9},{5... | collective-permute-start | bytes 884744 | tf_op jit(solution)/shard_map/ppermute | solution.py:329
  207.8 29.6 %collective-permute-start.12 = (bf16[512,768]{1,0:T(8,128)(2,1)S(1)}, bf16[512,768]{1,0:T(8,128)(2,1)S(1)}, u32[]{:S(2)}, u32[]{:S(2)}) collective-permute-start(bf16[512,768]{1,0:T(8,128)(2,1)S(1)} %get-tuple-element.30), channel_id=1, source_target_pairs={{0,2},{1,3},{2,0},{3,1},{4,6},{5,7},{6,4},{7,5},{8,10},{9,11},{10,... | collective-permute-start | bytes 2359304 | tf_op jit(solution)/shard_map/ppermute | solution.py:359
  208.3 6.8 %collective-permute-start.50 = (bf16[192,768]{1,0:T(8,128)(2,1)S(1)}, bf16[192,768]{1,0:T(8,128)(2,1)S(1)}, u32[]{:S(2)}, u32[]{:S(2)}) collective-permute-start(bf16[192,768]{1,0:T(8,128)(2,1)S(1)} %dynamic-slice_convert_fusion.3), channel_id=1, source_target_pairs={{0,4},{4,0},{8,12},{12,8},{16,20},{20,16},{24,28},{28,24},{1,5},{5... | collective-permute-start | bytes 884744 | tf_op jit(solution)/shard_map/ppermute | solution.py:329
  215.2 6.7 %collective-permute-start.51 = (bf16[96,768]{1,0:T(8,128)(2,1)S(1)}, bf16[96,768]{1,0:T(8,128)(2,1)S(1)}, u32[]{:S(2)}, u32[]{:S(2)}) collective-permute-start(bf16[96,768]{1,0:T(8,128)(2,1)S(1)} %dynamic-slice_convert_fusion.9), channel_id=1, source_target_pairs={{0,8},{4,12},{8,0},{12,4},{16,24},{20,28},{24,16},{28,20},{1,9},{5... | collective-permute-start | bytes 442376 | tf_op jit(solution)/shard_map/ppermute | solution.py:329
  216.8 7.8 %collective-permute-start.58 = (bf16[48,768]{1,0:T(8,128)(2,1)S(1)}, bf16[48,768]{1,0:T(8,128)(2,1)S(1)}, u32[]{:S(2)}, u32[]{:S(2)}) collective-permute-start(bf16[48,768]{1,0:T(8,128)(2,1)S(1)} %dynamic-slice_convert_fusion.17), channel_id=1, source_target_pairs={{0,16},{4,20},{8,24},{12,28},{16,0},{20,4},{24,8},{28,12},{1,17},{... | collective-permute-start | bytes 221192 | tf_op jit(solution)/shard_map/ppermute | solution.py:329
  230.7 7.3 %collective-permute-start.60 = (bf16[96,768]{1,0:T(8,128)(2,1)S(1)}, bf16[96,768]{1,0:T(8,128)(2,1)S(1)}, u32[]{:S(2)}, u32[]{:S(2)}) collective-permute-start(bf16[96,768]{1,0:T(8,128)(2,1)S(1)} %maximum_select_fusion.21), channel_id=1, source_target_pairs={{0,4},{4,0},{8,12},{12,8},{16,20},{20,16},{24,28},{28,24},{1,5},{5... | collective-permute-start | bytes 442376 | tf_op jit(solution)/shard_map/ppermute | solution.py:329
  237.4 48.3 %collective-permute-start.13 = (bf16[512,768]{1,0:T(8,128)(2,1)S(1)}, bf16[512,768]{1,0:T(8,128)(2,1)}, u32[]{:S(2)}, u32[]{:S(2)}) collective-permute-start(bf16[512,768]{1,0:T(8,128)(2,1)S(1)} %get-tuple-element.30), channel_id=1, source_target_pairs={{0,1},{1,0},{2,3},{3,2},{4,5},{5,4},{6,7},{7,6},{8,9},{9,8},{10,11... | collective-permute-start | bytes 2359304 | tf_op jit(solution)/shard_map/ppermute | solution.py:359
  237.4 48.3 %collective-permute-start.14 = (bf16[512,768]{1,0:T(8,128)(2,1)S(1)}, bf16[512,768]{1,0:T(8,128)(2,1)}, u32[]{:S(2)}, u32[]{:S(2)}) collective-permute-start(bf16[512,768]{1,0:T(8,128)(2,1)S(1)} %collective-permute-done.12), channel_id=1, source_target_pairs={{0,1},{1,0},{2,3},{3,2},{4,5},{5,4},{6,7},{7,6},{8,9},{9,8},{10,11... | collective-permute-start | bytes 2359304 | tf_op jit(solution)/shard_map/ppermute | solution.py:359
  238.0 44.6 %collective-permute-start.61 = (bf16[192,768]{1,0:T(8,128)(2,1)S(1)}, bf16[192,768]{1,0:T(8,128)(2,1)S(1)}, u32[]{:S(2)}, u32[]{:S(2)}) collective-permute-start(bf16[192,768]{1,0:T(8,128)(2,1)S(1)} %maximum_select_fusion.14), channel_id=1, source_target_pairs={{0,8},{4,12},{8,0},{12,4},{16,24},{20,28},{24,16},{28,20},{1,9},{5... | collective-permute-start | bytes 884744 | tf_op jit(solution)/shard_map/ppermute | solution.py:329
  240.2 42.7 %collective-permute-start.55 = (bf16[192,768]{1,0:T(8,128)(2,1)S(1)}, bf16[192,768]{1,0:T(8,128)(2,1)}, u32[]{:S(2)}, u32[]{:S(2)}) collective-permute-start(bf16[192,768]{1,0:T(8,128)(2,1)S(1)} %maximum_select_fusion.13), channel_id=1, source_target_pairs={{0,4},{4,0},{8,12},{12,8},{16,20},{20,16},{24,28},{28,24},{1,5},{5... | collective-permute-start | bytes 884744 | tf_op jit(solution)/shard_map/ppermute | solution.py:329
  282.6 73.9 %collective-permute-start.36 = (bf16[768,1536]{1,0:T(8,128)(2,1)}, bf16[768,1536]{1,0:T(8,128)(2,1)}, u32[]{:S(2)}, u32[]{:S(2)}) collective-permute-start(bf16[768,1536]{1,0:T(8,128)(2,1)} %add_convert_fusion), channel_id=1, source_target_pairs={{0,1},{1,0},{2,3},{3,2},{4,5},{5,4},{6,7},{7,6},{8,9},{9,8},{10,11... | collective-permute-start | bytes 7077896 | tf_op jit(solution)/shard_map/ppermute | solution.py:359
  346.2 139.4 %collective-permute-start.15 = (bf16[2,512,576]{1,2,0:T(8,128)(2,1)}, bf16[2,512,576]{1,2,0:T(8,128)(2,1)}, u32[]{:S(2)}, u32[]{:S(2)}) collective-permute-start(bf16[2,512,576]{1,2,0:T(8,128)(2,1)} %copy.36), channel_id=1, source_target_pairs={{0,1},{1,0},{2,3},{3,2},{4,5},{5,4},{6,7},{7,6},{8,9},{9,8},{10,11... | collective-permute-start | bytes 3538952 | tf_op jit(solution)/shard_map/ppermute | solution.py:359
  351.9 17.2 %collective-permute-start.24 = (bf16[192,576]{0,1:T(8,128)(2,1)S(1)}, bf16[192,576]{0,1:T(8,128)(2,1)S(1)}, u32[]{:S(2)}, u32[]{:S(2)}) collective-permute-start(bf16[192,576]{0,1:T(8,128)(2,1)S(1)} %dynamic-slice_convert_fusion.6), channel_id=1, source_target_pairs={{0,8},{4,12},{8,0},{12,4},{16,24},{20,28},{24,16},{28,20},{1,9},{5... | collective-permute-start | bytes 663560 | tf_op jit(solution)/shard_map/ppermute | solution.py:329
  352.6 18.9 %collective-permute-start.18 = (bf16[192,576]{0,1:T(8,128)(2,1)S(1)}, bf16[192,576]{0,1:T(8,128)(2,1)S(1)}, u32[]{:S(2)}, u32[]{:S(2)}) collective-permute-start(bf16[192,576]{0,1:T(8,128)(2,1)S(1)} %dynamic-slice_convert_fusion.7), channel_id=1, source_target_pairs={{0,4},{4,0},{8,12},{12,8},{16,20},{20,16},{24,28},{28,24},{1,5},{5... | collective-permute-start | bytes 663560 | tf_op jit(solution)/shard_map/ppermute | solution.py:329
  356.6 7.4 %collective-permute-start.30 = (bf16[96,768]{1,0:T(8,128)(2,1)S(1)}, bf16[96,768]{1,0:T(8,128)(2,1)S(1)}, u32[]{:S(2)}, u32[]{:S(2)}) collective-permute-start(bf16[96,768]{1,0:T(8,128)(2,1)S(1)} %dynamic-slice_convert_fusion.12), channel_id=1, source_target_pairs={{0,8},{4,12},{8,0},{12,4},{16,24},{20,28},{24,16},{28,20},{1,9},{5... | collective-permute-start | bytes 442376 | tf_op jit(solution)/shard_map/ppermute | solution.py:329
  368.8 87.4 %collective-permute-start.43 = (bf16[192,1536]{1,0:T(8,128)(2,1)S(1)}, bf16[192,1536]{1,0:T(8,128)(2,1)S(1)}, u32[]{:S(2)}, u32[]{:S(2)}) collective-permute-start(bf16[192,1536]{1,0:T(8,128)(2,1)S(1)} %dynamic-slice_convert_fusion), channel_id=1, source_target_pairs={{0,8},{4,12},{8,0},{12,4},{16,24},{20,28},{24,16},{28,20},{1,9},{5... | collective-permute-start | bytes 1769480 | tf_op jit(solution)/shard_map/ppermute | solution.py:329
  369.2 89.0 %collective-permute-start.37 = (bf16[192,1536]{1,0:T(8,128)(2,1)S(1)}, bf16[192,1536]{1,0:T(8,128)(2,1)S(1)}, u32[]{:S(2)}, u32[]{:S(2)}) collective-permute-start(bf16[192,1536]{1,0:T(8,128)(2,1)S(1)} %dynamic-slice_convert_fusion.1), channel_id=1, source_target_pairs={{0,4},{4,0},{8,12},{12,8},{16,20},{20,16},{24,28},{28,24},{1,5},{5... | collective-permute-start | bytes 1769480 | tf_op jit(solution)/shard_map/ppermute | solution.py:329
  371.5 9.3 %collective-permute-start.32 = (bf16[24,768]{1,0:T(8,128)(2,1)S(1)}, bf16[24,768]{1,0:T(8,128)(2,1)S(1)}, u32[]{:S(2)}, u32[]{:S(2)}) collective-permute-start(bf16[24,768]{1,0:T(8,128)(2,1)S(1)} %dynamic-slice_convert_fusion.20), channel_id=1, source_target_pairs={{0,16},{4,20},{8,24},{12,28},{16,0},{20,4},{24,8},{28,12},{1,17},{... | collective-permute-start | bytes 110600 | tf_op jit(solution)/shard_map/ppermute | solution.py:329
  401.1 9.2 %collective-permute-start.26 = (bf16[48,576]{0,1:T(8,128)(2,1)S(1)}, bf16[48,576]{0,1:T(8,128)(2,1)S(1)}, u32[]{:S(2)}, u32[]{:S(2)}) collective-permute-start(bf16[48,576]{0,1:T(8,128)(2,1)S(1)} %dynamic-slice_convert_fusion.13), channel_id=1, source_target_pairs={{0,16},{4,20},{8,24},{12,28},{16,0},{20,4},{24,8},{28,12},{1,17},{... | collective-permute-start | bytes 165896 | tf_op jit(solution)/shard_map/ppermute | solution.py:329
  410.3 9.3 %collective-permute-start.20 = (bf16[48,576]{0,1:T(8,128)(2,1)S(1)}, bf16[48,576]{0,1:T(8,128)(2,1)S(1)}, u32[]{:S(2)}, u32[]{:S(2)}) collective-permute-start(bf16[48,576]{0,1:T(8,128)(2,1)S(1)} %dynamic-slice_convert_fusion.15), channel_id=1, source_target_pairs={{0,16},{4,20},{8,24},{12,28},{16,0},{20,4},{24,8},{28,12},{1,17},{... | collective-permute-start | bytes 165896 | tf_op jit(solution)/shard_map/ppermute | solution.py:329
  419.6 8.9 %collective-permute-start.27 = (bf16[48,576]{0,1:T(8,128)(2,1)S(1)}, bf16[48,576]{0,1:T(8,128)(2,1)S(1)}, u32[]{:S(2)}, u32[]{:S(2)}) collective-permute-start(bf16[48,576]{0,1:T(8,128)(2,1)S(1)} %add_convert_fusion.10), channel_id=1, source_target_pairs={{0,16},{4,20},{8,24},{12,28},{16,0},{20,4},{24,8},{28,12},{1,17},{... | collective-permute-start | bytes 165896 | tf_op jit(solution)/shard_map/ppermute | solution.py:329
  428.5 7.2 %collective-permute-start.21 = (bf16[48,576]{0,1:T(8,128)(2,1)S(1)}, bf16[48,576]{0,1:T(8,128)(2,1)S(1)}, u32[]{:S(2)}, u32[]{:S(2)}) collective-permute-start(bf16[48,576]{0,1:T(8,128)(2,1)S(1)} %add_convert_fusion.11), channel_id=1, source_target_pairs={{0,16},{4,20},{8,24},{12,28},{16,0},{20,4},{24,8},{28,12},{1,17},{... | collective-permute-start | bytes 165896 | tf_op jit(solution)/shard_map/ppermute | solution.py:329
  435.7 6.6 %collective-permute-start.35 = (bf16[96,768]{1,0:T(8,128)(2,1)S(1)}, bf16[96,768]{1,0:T(8,128)(2,1)S(1)}, u32[]{:S(2)}, u32[]{:S(2)}) collective-permute-start(bf16[96,768]{1,0:T(8,128)(2,1)S(1)} %maximum_select_fusion.19), channel_id=1, source_target_pairs={{0,8},{4,12},{8,0},{12,4},{16,24},{20,28},{24,16},{28,20},{1,9},{5... | collective-permute-start | bytes 442376 | tf_op jit(solution)/shard_map/ppermute | solution.py:329
  442.3 6.6 %collective-permute-start.28 = (bf16[96,576]{0,1:T(8,128)(2,1)S(1)}, bf16[96,576]{0,1:T(8,128)(2,1)S(1)}, u32[]{:S(2)}, u32[]{:S(2)}) collective-permute-start(bf16[96,576]{0,1:T(8,128)(2,1)S(1)} %maximum_select_fusion.18), channel_id=1, source_target_pairs={{0,4},{4,0},{8,12},{12,8},{16,20},{20,16},{24,28},{28,24},{1,5},{5... | collective-permute-start | bytes 331784 | tf_op jit(solution)/shard_map/ppermute | solution.py:329
  455.4 9.7 %collective-permute-start.29 = (bf16[192,576]{0,1:T(8,128)(2,1)S(1)}, bf16[192,576]{0,1:T(8,128)(2,1)S(1)}, u32[]{:S(2)}, u32[]{:S(2)}) collective-permute-start(bf16[192,576]{0,1:T(8,128)(2,1)S(1)} %maximum_select_fusion.9), channel_id=1, source_target_pairs={{0,8},{4,12},{8,0},{12,4},{16,24},{20,28},{24,16},{28,20},{1,9},{5... | collective-permute-start | bytes 663560 | tf_op jit(solution)/shard_map/ppermute | solution.py:329
  456.3 9.3 %collective-permute-start.23 = (bf16[192,576]{0,1:T(8,128)(2,1)S(1)}, bf16[192,576]{0,1:T(8,128)(2,1)S(1)}, u32[]{:S(2)}, u32[]{:S(2)}) collective-permute-start(bf16[192,576]{0,1:T(8,128)(2,1)S(1)} %maximum_select_fusion.7), channel_id=1, source_target_pairs={{0,4},{4,0},{8,12},{12,8},{16,20},{20,16},{24,28},{28,24},{1,5},{5... | collective-permute-start | bytes 663560 | tf_op jit(solution)/shard_map/ppermute | solution.py:329
  458.2 9.1 %collective-permute-start.44 = (bf16[96,1536]{1,0:T(8,128)(2,1)S(1)}, bf16[96,1536]{1,0:T(8,128)(2,1)S(1)}, u32[]{:S(2)}, u32[]{:S(2)}) collective-permute-start(bf16[96,1536]{1,0:T(8,128)(2,1)S(1)} %dynamic-slice_convert_fusion.4), channel_id=1, source_target_pairs={{0,4},{4,0},{8,12},{12,8},{16,20},{20,16},{24,28},{28,24},{1,5},{5... | collective-permute-start | bytes 884744 | tf_op jit(solution)/shard_map/ppermute | solution.py:329
  465.1 9.7 %collective-permute-start.38 = (bf16[96,1536]{1,0:T(8,128)(2,1)S(1)}, bf16[96,1536]{1,0:T(8,128)(2,1)S(1)}, u32[]{:S(2)}, u32[]{:S(2)}) collective-permute-start(bf16[96,1536]{1,0:T(8,128)(2,1)S(1)} %dynamic-slice_convert_fusion.5), channel_id=1, source_target_pairs={{0,8},{4,12},{8,0},{12,4},{16,24},{20,28},{24,16},{28,20},{1,9},{5... | collective-permute-start | bytes 884744 | tf_op jit(solution)/shard_map/ppermute | solution.py:329
  467.8 7.7 %collective-permute-start.45 = (bf16[48,1536]{1,0:T(8,128)(2,1)S(1)}, bf16[48,1536]{1,0:T(8,128)(2,1)S(1)}, u32[]{:S(2)}, u32[]{:S(2)}) collective-permute-start(bf16[48,1536]{1,0:T(8,128)(2,1)S(1)} %dynamic-slice_convert_fusion.10), channel_id=1, source_target_pairs={{0,16},{4,20},{8,24},{12,28},{16,0},{20,4},{24,8},{28,12},{1,17},{... | collective-permute-start | bytes 442376 | tf_op jit(solution)/shard_map/ppermute | solution.py:329
  474.9 8.9 %collective-permute-start.39 = (bf16[48,1536]{1,0:T(8,128)(2,1)S(1)}, bf16[48,1536]{1,0:T(8,128)(2,1)S(1)}, u32[]{:S(2)}, u32[]{:S(2)}) collective-permute-start(bf16[48,1536]{1,0:T(8,128)(2,1)S(1)} %dynamic-slice_convert_fusion.11), channel_id=1, source_target_pairs={{0,16},{4,20},{8,24},{12,28},{16,0},{20,4},{24,8},{28,12},{1,17},{... | collective-permute-start | bytes 442376 | tf_op jit(solution)/shard_map/ppermute | solution.py:329
  475.7 14.5 %collective-permute-start.46 = (bf16[48,1536]{1,0:T(8,128)(2,1)S(1)}, bf16[48,1536]{1,0:T(8,128)(2,1)S(1)}, u32[]{:S(2)}, u32[]{:S(2)}) collective-permute-start(bf16[48,1536]{1,0:T(8,128)(2,1)S(1)} %add_convert_fusion.8), channel_id=1, source_target_pairs={{0,16},{4,20},{8,24},{12,28},{16,0},{20,4},{24,8},{28,12},{1,17},{... | collective-permute-start | bytes 442376 | tf_op jit(solution)/shard_map/ppermute | solution.py:329
  484.8 7.4 %collective-permute-start.40 = (bf16[48,1536]{1,0:T(8,128)(2,1)S(1)}, bf16[48,1536]{1,0:T(8,128)(2,1)}, u32[]{:S(2)}, u32[]{:S(2)}) collective-permute-start(bf16[48,1536]{1,0:T(8,128)(2,1)S(1)} %add_convert_fusion.9), channel_id=1, source_target_pairs={{0,16},{4,20},{8,24},{12,28},{16,0},{20,4},{24,8},{28,12},{1,17},{... | collective-permute-start | bytes 442376 | tf_op jit(solution)/shard_map/ppermute | solution.py:329
  488.6 28.6 %collective-permute-start.17 = (bf16[512,768]{1,0:T(8,128)(2,1)}, bf16[512,768]{1,0:T(8,128)(2,1)}, u32[]{:S(2)}, u32[]{:S(2)}) collective-permute-start(bf16[512,768]{1,0:T(8,128)(2,1)} %add_convert_fusion.3), channel_id=1, source_target_pairs={{0,2},{1,3},{2,0},{3,1},{4,6},{5,7},{6,4},{7,5},{8,10},{9,11},{10,... | collective-permute-start | bytes 2359304 | tf_op jit(solution)/shard_map/ppermute | solution.py:359
  490.3 15.1 %collective-permute-start.47 = (bf16[96,1536]{1,0:T(8,128)(2,1)S(1)}, bf16[96,1536]{1,0:T(8,128)(2,1)S(1)}, u32[]{:S(2)}, u32[]{:S(2)}) collective-permute-start(bf16[96,1536]{1,0:T(8,128)(2,1)S(1)} %maximum_select_fusion.12), channel_id=1, source_target_pairs={{0,4},{4,0},{8,12},{12,8},{16,20},{20,16},{24,28},{28,24},{1,5},{5... | collective-permute-start | bytes 884744 | tf_op jit(solution)/shard_map/ppermute | solution.py:329
  494.0 13.2 %collective-permute-start.41 = (bf16[96,1536]{1,0:T(8,128)(2,1)}, bf16[96,1536]{1,0:T(8,128)(2,1)S(1)}, u32[]{:S(2)}, u32[]{:S(2)}) collective-permute-start(bf16[96,1536]{1,0:T(8,128)(2,1)} %maximum_select_fusion.11), channel_id=1, source_target_pairs={{0,8},{4,12},{8,0},{12,4},{16,24},{20,28},{24,16},{28,20},{1,9},{5... | collective-permute-start | bytes 884744 | tf_op jit(solution)/shard_map/ppermute | solution.py:329
  506.3 14.0 %collective-permute-start.48 = (bf16[192,1536]{1,0:T(8,128)(2,1)}, bf16[192,1536]{1,0:T(8,128)(2,1)}, u32[]{:S(2)}, u32[]{:S(2)}) collective-permute-start(bf16[192,1536]{1,0:T(8,128)(2,1)} %maximum_select_fusion.1), channel_id=1, source_target_pairs={{0,8},{4,12},{8,0},{12,4},{16,24},{20,28},{24,16},{28,20},{1,9},{5... | collective-permute-start | bytes 1769480 | tf_op jit(solution)/shard_map/ppermute | solution.py:329
  509.1 17.6 %collective-permute-start.42 = (bf16[192,1536]{1,0:T(8,128)(2,1)}, bf16[192,1536]{1,0:T(8,128)(2,1)}, u32[]{:S(2)}, u32[]{:S(2)}) collective-permute-start(bf16[192,1536]{1,0:T(8,128)(2,1)} %maximum_select_fusion), channel_id=1, source_target_pairs={{0,4},{4,0},{8,12},{12,8},{16,20},{20,16},{24,28},{28,24},{1,5},{5... | collective-permute-start | bytes 1769480 | tf_op jit(solution)/shard_map/ppermute | solution.py:329
  (45 other events, 272.1 us)

commit v2 on v1

--- a/solution.py
+++ b/solution.py
@@ -22,6 +22,7 @@
 TN = (((0,), (0,)), ((), ()))
 NN = (((1,), (0,)), ((), ()))
 VMEM_LIMIT = 58 << 20
+MESH = pl.DeviceIdType.MESH
 
 
 def mm(a, b, dims=NN):
@@ -322,24 +323,178 @@
     return jnp.cos(angles), jnp.sin(angles) * sign[None, :]
 
 
-def reduce_over_dp(total, bits, me):
+def dp_orders(size):
+    bits = list(range(size.bit_length() - 1))
+    return [bits, bits[1::-1] + bits[2:]]
+
+
+def piece_rows(rows, size):
+    return -(-rows // (16 * size)) * 16
+
+
+def peer_of(index, bit):
+    mine = (index // (1 << bit)) % 2
+    return index + (1 - 2 * mine) * (1 << bit), mine
+
+
+def finish_kernel(
+    size, x_ref, dq_ref, w_ref, w_near_ref, dh_ref, norms_ref,
+    dx_ref, grad_ref, sums_ref,
+    total, give, take, near, far_out, far_in, own, norm_in,
+    near_sem, far_sem, give_sem, gather_sem, norm_sem,
+):
+    orders = dp_orders(size)
+    rows = total.shape[1] // size
+    cols = total.shape[2]
+    half = x_ref.shape[2] // 2
+    m, me = lax.axis_index("mp"), lax.axis_index("dp")
+    core, far = peer_of(m, 0)[0], peer_of(m, 1)[0]
+    stages = len(orders[0])
+
+    barrier = pltpu.get_barrier_semaphore()
+    partners = [{"mp": core}, {"mp": far}] + [{"dp": peer_of(me, bit)[0]} for bit in range(stages)]
+    for partner in partners:
+        pl.semaphore_signal(barrier, inc=1, device_id=partner, device_id_type=MESH)
+    pl.semaphore_wait(barrier, len(partners))
+
+    def send(source, target, sems, where, partner):
+        copy = pltpu.make_async_remote_copy(
+            source, target, sems.at[0, *where], sems.at[1, *where], device_id=partner, device_id_type=MESH
+        )
+        copy.start()
+        return copy
+
+    near_copy = send(dq_ref.at[pl.ds(2, 2)], near, near_sem, (), {"mp": core})
+    sums_ref[...] = norms_ref[...]
+    norm_partners = partners
+
+    for chain in range(2):
+        if total.shape[1] > half:
+            total[chain, half:, :] = jnp.zeros((total.shape[1] - half, cols), F32)
+        for part in range(0, half, LANES):
+            at = chain * half + part
+            piece = mm(x_ref[0, :, at : at + LANES], dq_ref[0], TN)
+            for slot in range(1, x_ref.shape[0]):
+                piece += mm(x_ref[slot, :, at : at + LANES], dq_ref[slot], TN)
+            total[chain, part : part + LANES, :] = piece
+
+    def scatter(stage, lows, count):
+        half_count = count // 2
+        copies, keeps = [], []
+        for chain in range(2):
+            partner, mine = peer_of(me, orders[chain][stage])
+            out = pl.ds(pl.multiple_of((lows[chain] + (1 - mine) * half_count) * rows, 16), half_count * rows)
+            keeps.append(lows[chain] + mine * half_count)
+            spot = pl.ds(half_count * rows, half_count * rows)
+            give[chain, spot, :] = total[chain, out, :].astype(BF16)
+            copies.append(
+                send(give.at[chain, spot], take.at[chain, spot], give_sem, (chain, stage), {"dp": partner})
+            )
+        return copies, keeps
+
+    def absorb(copies, keeps, count):
+        half_count = count // 2
+        for chain in range(2):
+            copies[chain].wait()
+            keep = pl.ds(pl.multiple_of(keeps[chain] * rows, 16), half_count * rows)
+            total[chain, keep, :] += take[chain, pl.ds(half_count * rows, half_count * rows), :].astype(F32)
+
+    def norm_exchange(stage):
+        return send(sums_ref, norm_in.at[stage], norm_sem, (stage,), norm_partners[stage])
+
+    def norm_add(stage, copy):
+        copy.wait()
+        sums_ref[...] += norm_in[stage]
+
+    lows, count = [0, 0], size
+    copies, keeps = scatter(0, lows, count)
+    norm_copy = norm_exchange(0)
+    near_copy.wait()
+    d_far = mm(dq_ref[1], w_ref[...], NT) + mm(near[1], w_near_ref[...], NT)
+    far_out[...] = d_far.astype(BF16)
+    far_copy = send(far_out, far_in, far_sem, (), {"mp": far})
+    d_own = mm(dq_ref[0], w_ref[...], NT) + mm(near[0], w_near_ref[...], NT)
+    own[...] = dh_ref[...] + d_own
+    norm_add(0, norm_copy)
+    norm_done = 1
+    for stage in range(stages):
+        norm_copy = norm_exchange(norm_done) if norm_done < len(partners) else None
+        absorb(copies, keeps, count)
+        lows, count = keeps, count // 2
+        if stage + 1 < stages:
+            copies, keeps = scatter(stage + 1, lows, count)
+        if norm_copy is not None:
+            norm_add(norm_done, norm_copy)
+            norm_done += 1
+    for chain in range(2):
+        mine = pl.ds(pl.multiple_of(lows[chain] * rows, 16), rows)
+        grad_ref[chain, mine, :] = total[chain, mine, :].astype(BF16)
+    for stage in reversed(range(stages)):
+        copies = []
+        for chain in range(2):
+            partner, mine = peer_of(me, orders[chain][stage])
+            block = pl.ds(pl.multiple_of(lows[chain] * rows, 16), count * rows)
+            spot = grad_ref.at[chain, block]
+            copies.append(send(spot, spot, gather_sem, (chain, stage), {"dp": partner}))
+            lows[chain] = lows[chain] - mine * count
+        if norm_done < len(partners):
+            norm_add(norm_done, norm_exchange(norm_done))
+            norm_done += 1
+        for copy in copies:
+            copy.wait()
+        count *= 2
+    far_copy.wait()
+    dx_ref[...] = (own[...] + far_in[...].astype(F32)).astype(BF16)
+    while norm_done < len(partners):
+        norm_add(norm_done, norm_exchange(norm_done))
+        norm_done += 1
+
+
+def finish(x_slots, d_qkv, w_qkv, w_near, dh, norms):
     size = lax.axis_size("dp")
-
-    def exchange(values, bit):
-        return lax.ppermute(values, "dp", [(i, i ^ (1 << bit)) for i in range(size)])
-
-    for bit in bits:
-        half = total.shape[0] // 2
-        mine = (me >> bit) & 1
-        give = lax.dynamic_slice_in_dim(total, (1 - mine) * half, half, 0).astype(BF16)
-        keep = lax.dynamic_slice_in_dim(total, mine * half, half, 0)
-        total = keep + exchange(give, bit).astype(F32)
-    total = total.astype(BF16)
-    for bit in reversed(bits):
-        mine = (me >> bit) & 1
-        other = exchange(total, bit)
-        total = jnp.where(mine == 0, jnp.concatenate([total, other]), jnp.concatenate([other, total]))
-    return total
+    stages = size.bit_length() - 1
+    slots, rows, width = x_slots.shape
+    cols = d_qkv.shape[2]
+    padded = piece_rows(width // 2, size) * size
+    vmem = pl.BlockSpec(memory_space=pltpu.VMEM)
+    dma = pltpu.SemaphoreType.DMA
+    return pl.pallas_call(
+        functools.partial(finish_kernel, size),
+        out_shape=(
+            jax.ShapeDtypeStruct((rows, width), BF16),
+            jax.ShapeDtypeStruct((2, padded, cols), BF16),
+            jax.ShapeDtypeStruct(norms.shape, F32),
+        ),
+        in_specs=[vmem] * 6,
+        out_specs=[vmem] * 3,
+        scratch_shapes=[
+            pltpu.VMEM((2, padded, cols), F32),
+            pltpu.VMEM((2, padded, cols), BF16),
+            pltpu.VMEM((2, padded, cols), BF16),
+            pltpu.VMEM((2, rows, cols), BF16),
+            pltpu.VMEM((rows, width), BF16),
+            pltpu.VMEM((rows, width), BF16),
+            pltpu.VMEM((rows, width), F32),
+            pltpu.VMEM((2 + stages,) + norms.shape, F32),
+            dma((2,)),
+            dma((2,)),
+            dma((2, 2, stages)),
+            dma((2, 2, stages)),
+            dma((2, 2 + stages)),
+        ],
+        compiler_params=pltpu.CompilerParams(
+            collective_id=1, has_side_effects=True, vmem_limit_bytes=VMEM_LIMIT
+        ),
+        cost_estimate=pl.CostEstimate(
+            flops=6 * slots * rows * width * cols, bytes_accessed=12 * rows * width, transcendentals=0
+        ),
+        name="finish",
+    )(x_slots, d_qkv, w_qkv, w_near, dh, norms)
+
+
+def sum_over_dp(values):
+    piece = lax.psum_scatter(values.astype(BF16), "dp", scatter_dimension=0, tiled=True)
+    return lax.all_gather(piece, "dp", axis=0, tiled=True).astype(F32)
 
 
 def body(
@@ -352,8 +507,6 @@
     heads = local_cols // HEAD_DIM
     hidden_cols = w_down.shape[0]
     m = lax.axis_index("mp")
-    dp_bits = list(range(int(math.log2(lax.axis_size("dp")))))
-    me = lax.axis_index("dp")
 
     def swap(values, distance):
         return lax.ppermute(values, "mp", [(i, i ^ distance) for i in range(shards)])
@@ -444,17 +597,8 @@
     grad_gate_up, grad_down = weight_grads(0)
     grad_gate_up = grad_gate_up + grad_gate_up_near.astype(F32)
     grad_down = grad_down + grad_down_near.astype(F32)
-    swapped = [dp_bits[1], dp_bits[0]] + dp_bits[2:] if len(dp_bits) > 1 else dp_bits
-    half = width // 2
-    grad_gate_up = jnp.concatenate(
-        [reduce_over_dp(grad_gate_up[:half], dp_bits, me), reduce_over_dp(grad_gate_up[half:], swapped, me)]
-    ).astype(F32)
-    grad_down = jnp.concatenate(
-        [
-            reduce_over_dp(grad_down[: hidden_cols // 2], dp_bits, me),
-            reduce_over_dp(grad_down[hidden_cols // 2 :], swapped, me),
-        ]
-    ).astype(F32)
+    grad_gate_up = sum_over_dp(grad_gate_up)
+    grad_down = sum_over_dp(grad_down)
 
     d_normed = dz + d_own + d_normed_far.astype(F32)
     e1 = d_normed * ln1_scale
@@ -467,17 +611,11 @@
     dh_slots = jnp.stack([dh_low, dh_far, dh_near, dh_last])
     d_qkv = attend_back(qb, k, v, att, dh_slots, w_out, cosine, sine, place, ranges)
     grad_out = mm(att.reshape(length, local_cols), dh_slots.reshape(length, width), TN)
-    d_qkv_near = beside(d_qkv[2:])
-    d_x_far = mm(d_qkv[1], flat_qkv, NT) + mm(d_qkv_near[1], w_qkv_near, NT)
-    d_x_far = across(d_x_far.astype(BF16))
-    d_x_own = mm(d_qkv[0], flat_qkv, NT) + mm(d_qkv_near[0], w_qkv_near, NT)
-    grad_qkv = mm(x_slots.reshape(length, width), d_qkv.reshape(length, 3 * local_cols), TN)
-    d_tokens = (dh + d_x_own + d_x_far.astype(F32)).astype(BF16)
-    grad_qkv = jnp.concatenate(
-        [reduce_over_dp(grad_qkv[:half], dp_bits, me), reduce_over_dp(grad_qkv[half:], swapped, me)]
-    ).astype(F32)
-    grad_out = reduce_over_dp(grad_out, swapped, me).astype(F32)
-    norms = lax.psum(jnp.stack([d_scale_one, d_shift_one, d_scale_two, d_shift_two]), ("dp", "mp"))
+    grad_out = sum_over_dp(grad_out)
+    norms = jnp.stack([d_scale_one, d_shift_one, d_scale_two, d_shift_two])
+    norms = jnp.concatenate([norms, jnp.zeros_like(norms)])
+    d_tokens, grad_qkv, norms = finish(x_slots, d_qkv, flat_qkv, w_qkv_near, dh, norms)
+    grad_qkv = grad_qkv[:, : width // 2].reshape(width, 3 * local_cols).astype(F32)
     norms = lax.dynamic_slice_in_dim(norms, m * local_cols, local_cols, 1)
     return (
         output,

time: 542 us -> 508 us (0.937)
  Pallas kernels: 104 us -> 172 us
  starting transfers between devices: 67.2 us -> 15.8 us
  other arithmetic: 63.4 us -> 28.3 us
  matrix products: 69.9 us -> 42.7 us
  between operations: 1.94 us -> 14.9 us
  blocking collectives: 40.2 us -> 32.1 us
  waiting for transfers between devices: 166 us -> 174 us
    ppermute x42 -> x0, waiting for transfers between devices: 103 us -> none  [exchange(): return lax.ppermute(values, 'dp', [(i, i ^ 1 << bit) for i in range(size)])]
    reduce_scatter x0 -> x3, waiting for transfers between devices: none -> 71.9 us  [sum_over_dp(): lax.psum_scatter(values.astype(BF16), 'dp', scatter_dimension=0, tiled=True)]
    pallas_call x0 -> x1, Pallas kernels: none -> 67.8 us  [finish(): pl.pallas_call(functools.partial(finish_kernel, size), out_shape=(jax.Sha...]
    ppermute x42 -> x0, starting transfers between devices: 51.3 us -> none  [exchange(): return lax.ppermute(values, 'dp', [(i, i ^ 1 << bit) for i in range(size)])]
    psum x1 -> x0, blocking collectives: 40.2 us -> none  [body(): lax.psum(jnp.stack([d_scale_one, d_shift_one, d_scale_two, d_shift_two]),...]
    ppermute x20 -> x18, waiting for transfers between devices: 63 us -> 102 us  [swap(): lax.ppermute(values, 'mp', [(i, i ^ distance) for i in range(shards)])]
    all_gather x0 -> x1, blocking collectives: none -> 32.1 us  [sum_over_dp(): return lax.all_gather(piece, 'dp', axis=0, tiled=True).astype(F32)]
    dot_general x34 -> x29, matrix products: 69.9 us -> 42.7 us  [mm(): return lax.dot_general(a, b, dims, preferred_element_type=F32)]
  transfers between devices with their start and end apart: 62 -> 23, of which waited for: 33 -> 12; matrix products, arithmetic and copies ran while one was open for 26% -> 16% of each run, Pallas kernels for 10% -> 24%
where the time goes in v2:
time: 508 us; the launch traced here: 505 us
  waiting for transfers between devices  174 us (34%)
  Pallas kernels  172 us (34%)
  matrix products  42.7 us (8%)
  blocking collectives  32.1 us (6%)
  other arithmetic  28.3 us (6%)
  local copies, waits for them, and re-layouts  25.6 us (5%)
  starting transfers between devices  15.8 us (3%)
  between operations  14.9 us (3%)
    ppermute x18, waiting for transfers between devices, swap(): lax.ppermute(values, 'mp', [(i, i ^ distance) for i in range(shards)])  102 us
    reduce_scatter x3, waiting for transfers between devices, sum_over_dp(): lax.psum_scatter(values.astype(BF16), 'dp', scatter_dimension=0, tiled=True)  71.9 us
    pallas_call x1, Pallas kernels, finish(): pl.pallas_call(functools.partial(finish_kernel, size), out_shape=(jax.Sha...  67.8 us
    pallas_call x1, Pallas kernels, attend_back(): pl.pallas_call(attend_back_kernel, out_shape=jax.ShapeDtypeStruct((shards...  54.6 us
    dot_general x29, matrix products, mm(): return lax.dot_general(a, b, dims, preferred_element_type=F32)  42.7 us
    pallas_call x1, Pallas kernels, attend(): pl.pallas_call(attend_kernel, out_shape=(jax.ShapeDtypeStruct((shards, ro...  39.5 us
    all_gather x1, blocking collectives, sum_over_dp(): return lax.all_gather(piece, 'dp', axis=0, tiled=True).astype(F32)  32.1 us
    ppermute x18, starting transfers between devices, swap(): lax.ppermute(values, 'mp', [(i, i ^ distance) for i in range(shards)])  15.2 us
  transfers between devices with their start and end apart: 23, of which 12 were waited for; matrix products, arithmetic and copies ran while one was open for 16% of the time, Pallas kernels for 24%

profile of v2, /device:TPU:0, one launch (start us, length us, event | category | flops | bytes accessed | tf_op | source)
XLA Modules:
  0.0 505.3 jit_solution(10817181251896545283)
XLA Ops:
  7.2 3.0 collective-permute-start
  11.2 2.3 copy.38.w_ref
  15.2 12.9 %collective-permute-done = bf16[512,768]{1,0:T(8,128)(2,1)S(1)} collective-permute-done((bf16[512,768]{1,0:T(8,128)(2,1)}, bf16[512,768]{1,0:T(8,128)(2,1)S(1)}, u32[]{:S(2)}, u32[]{:S(2)}) %collective-permute-start) | collective-permute-done | bytes 786464 | tf_op jit(solution)/shard_map/ppermute | solution.py:512
  28.6 5.5 %fusion.45 = (f32[2048,128]{1,0:T(8,128)}, f32[2048,128]{1,0:T(8,128)}) fusion(f32[128]{0:T(128)S(1)} %get-tuple-element.78, f32[128]{0:T(128)S(1)} %get-tuple-element.79, f32[2048]{0:T(1024)S(1)} %subtract_convert_fusion), kind=kLoop, calls=%fused_computation.93 | loop fusion | flops 524288 | bytes 2106368 | tf_op jit(solution)/shard_map/mul | solution.py:323
  34.2 1.9 pad_maximum_fusion.x_ref
  36.1 10.3 %project.1 = (bf16[3,2048,128]{2,1,0:T(8,128)(2,1)}, bf16[3,2048,128]{2,1,0:T(8,128)(2,1)}, bf16[3,2048,128]{2,1,0:T(8,128)(2,1)}) custom-call(s32[5]{0:T(128)} %stack.58.place, bf16[4,512,768]{2,1,0:T(8,128)(2,1)} %pad_maximum_fusion.x_ref, bf16[768,576]{1,0:T(8,128)(2,1)} %copy.38.w_ref, f32[2048,128]{1,0:T(8,128)} %get-tuple-element.67.cos_ref, ...), custom_call_target="tpu_custom_call" | custom-call | flops 1811939328 | bytes 7864320 | tf_op jit(solution)/shard_map/project/pallas_call | solution.py:101
  46.3 39.5 %attend.1 = (bf16[4,512,192]{2,1,0:T(8,128)(2,1)}, bf16[3,2048,128]{2,1,0:T(8,128)(2,1)}) custom-call(s32[5]{0:T(128)} %stack.58.place, s32[16]{0:T(128)} %pad_add_fusion.1.ranges, bf16[3,2048,128]{2,1,0:T(8,128)(2,1)} %get-tuple-element.18.q_ref, bf16[3,2048,128]{2,1,0:T(8,128)(2,1)} %get-tuple-element.19.k_ref, bf16[3,2048,128]{2,1,0:T(8,128)(2,1)} %get-tuple-element.20.v_ref), custom_call_target="tpu_custom_call" | custom-call | flops 4831838208 | bytes 7864320 | tf_op jit(solution)/shard_map/attend/pallas_call | solution.py:175
  89.8 1.8 collective-permute-start.5
  94.7 15.0 %collective-permute-done.5 = bf16[512,768]{1,0:T(8,128)(2,1)S(1)} collective-permute-done((bf16[512,768]{1,0:T(8,128)(2,1)S(1)}, bf16[512,768]{1,0:T(8,128)(2,1)S(1)}, u32[]{:S(2)}, u32[]{:S(2)}) %collective-permute-start.5) | collective-permute-done | bytes 786464 | tf_op jit(solution)/shard_map/ppermute | solution.py:512
  111.2 1.8 collective-permute-start.8
  113.0 1.4 fusion.76
  114.9 1.4 fusion.77
  116.3 14.0 %collective-permute-done.8 = bf16[512,768]{1,0:T(8,128)(2,1)S(1)} collective-permute-done((bf16[512,768]{1,0:T(8,128)(2,1)S(1)}, bf16[512,768]{1,0:T(8,128)(2,1)S(1)}, u32[]{:S(2)}, u32[]{:S(2)}) %collective-permute-start.8) | collective-permute-done | bytes 786464 | tf_op jit(solution)/shard_map/ppermute | solution.py:512
  130.3 2.5 fusion.74
  134.1 1.4 fusion.75
  136.8 1.8 collective-permute-start.9
  140.6 14.3 %collective-permute-done.9 = bf16[512,768]{1,0:T(8,128)(2,1)S(1)} collective-permute-done((bf16[512,768]{1,0:T(8,128)(2,1)S(1)}, bf16[512,768]{1,0:T(8,128)(2,1)S(1)}, u32[]{:S(2)}, u32[]{:S(2)}) %collective-permute-start.9) | collective-permute-done | bytes 786464 | tf_op jit(solution)/shard_map/ppermute | solution.py:512
  158.3 1.8 collective-permute-start.10
  162.1 1.4 fusion.48
  164.4 2.4 fusion.12
  166.7 8.8 %collective-permute-done.10 = bf16[512,768]{1,0:T(8,128)(2,1)S(1)} collective-permute-done((bf16[512,768]{1,0:T(8,128)(2,1)S(1)}, bf16[512,768]{1,0:T(8,128)(2,1)S(1)}, u32[]{:S(2)}, u32[]{:S(2)}) %collective-permute-start.10) | collective-permute-done | bytes 786464 | tf_op jit(solution)/shard_map/ppermute | solution.py:512
  177.7 3.0 add_convert_fusion.1
  182.0 1.5 add_convert_fusion.2
  183.8 3.2 fusion.50
  188.2 1.4 fusion.46
  189.9 2.6 fusion.47
  192.4 4.6 add_convert_fusion
  197.2 4.2 add_convert_fusion.4
  201.4 1.8 collective-permute-start.11
  203.2 1.4 fusion.51
  204.6 1.4 fusion.49
  206.0 14.9 %collective-permute-done.11 = bf16[512,768]{1,0:T(8,128)(2,1)S(1)} collective-permute-done((bf16[512,768]{1,0:T(8,128)(2,1)S(1)}, bf16[512,768]{1,0:T(8,128)(2,1)S(1)}, u32[]{:S(2)}, u32[]{:S(2)}) %collective-permute-start.11) | collective-permute-done | bytes 786464 | tf_op jit(solution)/shard_map/ppermute | solution.py:512
  221.0 2.5 multiply_reduce_fusion
  223.5 1.6 fusion.70
  225.1 1.7 collective-permute-start.12
  226.8 17.0 %collective-permute-done.12 = bf16[512,768]{1,0:T(8,128)(2,1)S(1)} collective-permute-done((bf16[512,768]{1,0:T(8,128)(2,1)S(1)}, bf16[512,768]{1,0:T(8,128)(2,1)S(1)}, u32[]{:S(2)}, u32[]{:S(2)}) %collective-permute-start.12) | collective-permute-done | bytes 786464 | tf_op jit(solution)/shard_map/ppermute | solution.py:512
  243.8 2.3 collective-permute-done.14
  247.3 1.7 fusion.44
  250.2 71.1 %reduce-scatter.6.cloned.1.call-done = bf16[96,1536]{1,0:T(8,128)(2,1)} async-done(((bf16[768,1536]{1,0:T(8,128)(2,1)}), bf16[96,1536]{1,0:T(8,128)(2,1)}) %reduce-scatter.6.cloned.1.call-update) | async-done | bytes 294928 | tf_op jit(solution)/shard_map/reduce_scatter | solution.py:496
  322.3 1.8 collective-permute-done.15
  326.1 54.6 %attend_back.1.dq_ref = bf16[4,512,576]{2,1,0:T(8,128)(2,1)} custom-call(s32[5]{0:T(128)} %stack.58.place, s32[16]{0:T(128)} %pad_add_fusion.1.ranges, bf16[3,2048,128]{2,1,0:T(8,128)(2,1)} %get-tuple-element.22.qb_ref, bf16[3,2048,128]{2,1,0:T(8,128)(2,1)} %get-tuple-element.19.k_ref, bf16[3,2048,128]{2,1,0:T(8,128)(2,1)} %get-tuple-element.20.v_ref, ...), custom_call_target="tpu_custom_call" | custom-call | flops 8053063680 | bytes 9437184 | tf_op jit(solution)/shard_map/attend_back/pallas_call | solution.py:281
  380.6 67.8 %finish.1 = (bf16[512,768]{1,0:T(8,128)(2,1)}, bf16[2,384,576]{2,1,0:T(8,128)(2,1)}, f32[8,768]{1,0:T(8,128)}) custom-call(bf16[4,512,768]{2,1,0:T(8,128)(2,1)} %pad_maximum_fusion.x_ref, bf16[4,512,576]{2,1,0:T(8,128)(2,1)} %attend_back.1.dq_ref, bf16[768,576]{1,0:T(8,128)(2,1)} %copy.38.w_ref, bf16[768,576]{1,0:T(8,128)(2,1)} %copy.40.w_near_ref, ...), custom_call_target="tpu_custom_call" | custom-call | flops 5435817984 | bytes 4718592 | tf_op jit(solution)/shard_map/finish/pallas_call | solution.py:461
  448.5 2.6 copy.41
  451.1 2.6 reshape.135
  453.7 1.5 fusion.73
  455.2 32.1 %all_gather.9 = bf16[192,768]{1,0:T(8,128)(2,1)S(1)} all-gather(bf16[24,768]{1,0:T(8,128)(2,1)} %reduce-scatter.4.cloned.1.call-done), channel_id=1, replica_groups=mesh['dp'=8,'mp'=4] {'dp'}, dimensions={0}, use_global_device_ids=true | all-gather | bytes 331776 | tf_op jit(solution)/shard_map/all_gather | solution.py:497
  488.3 2.8 convert_element_type.207
  491.1 6.3 %reshape.137 = f32[768,2,768]{2,1,0:T(2,128)} reshape(bf16[768,1536]{1,0:T(8,128)(2,1)} %all-gather.3.cloned.1.call-done) | data formatting | bytes 7077888 | tf_op jit(solution)/shard_map/reshape | solution.py:625
  (166 shorter events, 35.0 us)
Async XLA Ops:
  7.2 6.3 %copy-start.29 = (s32[1,16]{1,0:T(1,128)S(1)}, s32[1,16]{1,0:T(1,128)}, u32[]{:S(2)}) copy-start(s32[1,16]{1,0:T(1,128)} %param.12) | copy-start | bytes 196
  7.2 242.7 %reduce-scatter.8.cloned.1.call-start = ((), (), s32[]{:S(2)}) async-start(), calls=%async_computation.6 | async-start | bytes 1327104 | tf_op jit(solution)/shard_map/reduce_scatter | solution.py:496
  7.2 20.8 %collective-permute-start = (bf16[512,768]{1,0:T(8,128)(2,1)}, bf16[512,768]{1,0:T(8,128)(2,1)S(1)}, u32[]{:S(2)}, u32[]{:S(2)}) collective-permute-start(bf16[512,768]{1,0:T(8,128)(2,1)} %param.11), channel_id=1, source_target_pairs={{0,2},{1,3},{2,0},{3,1},{4,6},{5,7},{6,4},{7,5},{8,10},{9,11},{10,... | collective-permute-start | bytes 2359304 | tf_op jit(solution)/shard_map/ppermute | solution.py:512
  10.3 23.9 %collective-permute-start.1 = (bf16[512,768]{1,0:T(8,128)(2,1)}, bf16[512,768]{1,0:T(8,128)(2,1)S(1)}, u32[]{:S(2)}, u32[]{:S(2)}) collective-permute-start(bf16[512,768]{1,0:T(8,128)(2,1)} %param.11), channel_id=1, source_target_pairs={{0,1},{1,0},{2,3},{3,2},{4,5},{5,4},{6,7},{7,6},{8,9},{9,8},{10,11... | collective-permute-start | bytes 2359304 | tf_op jit(solution)/shard_map/ppermute | solution.py:512
  11.2 23.0 %copy-start.12 = (bf16[512,768]{1,0:T(8,128)(2,1)S(1)}, bf16[512,768]{1,0:T(8,128)(2,1)}, u32[]{:S(2)}) copy-start(bf16[512,768]{1,0:T(8,128)(2,1)} %param.11) | copy-start | bytes 2359300
  28.0 6.1 %collective-permute-start.2 = (bf16[512,768]{1,0:T(8,128)(2,1)S(1)}, bf16[512,768]{1,0:T(8,128)(2,1)S(1)}, u32[]{:S(2)}, u32[]{:S(2)}) collective-permute-start(bf16[512,768]{1,0:T(8,128)(2,1)S(1)} %collective-permute-done), channel_id=1, source_target_pairs={{0,1},{1,0},{2,3},{3,2},{4,5},{5,4},{6,7},{7,6},{8,9},{9,8},{10,11... | collective-permute-start | bytes 2359304 | tf_op jit(solution)/shard_map/ppermute | solution.py:512
  46.3 41.1 %copy-start.15 = (bf16[192,768]{1,0:T(8,128)(2,1)S(1)}, bf16[192,768]{1,0:T(8,128)(2,1)}, u32[]{:S(2)}) copy-start(bf16[192,768]{1,0:T(8,128)(2,1)} %param.14) | copy-start | bytes 884740
  86.9 2.5 collective-permute-start.3
  87.5 2.0 collective-permute-start.4
  88.9 2.8 copy-start.16
  89.8 19.9 %collective-permute-start.5 = (bf16[512,768]{1,0:T(8,128)(2,1)S(1)}, bf16[512,768]{1,0:T(8,128)(2,1)S(1)}, u32[]{:S(2)}, u32[]{:S(2)}) collective-permute-start(bf16[512,768]{1,0:T(8,128)(2,1)S(1)} %add_convert_fusion.7), channel_id=1, source_target_pairs={{0,2},{1,3},{2,0},{3,1},{4,6},{5,7},{6,4},{7,5},{8,10},{9,11},{10,... | collective-permute-start | bytes 2359304 | tf_op jit(solution)/shard_map/ppermute | solution.py:512
  92.1 38.2 %copy-start = (bf16[96,8,2,768]{3,1,2,0:T(8,128)(2,1)}, bf16[96,8,2,768]{3,1,2,0:T(8,128)(2,1)S(1)}, u32[]{:S(2)}) copy-start(bf16[96,8,2,768]{3,1,2,0:T(8,128)(2,1)S(1)} %copy.44) | copy-start | bytes 7077892
  92.1 22.8 %collective-permute-start.6 = (bf16[768,1536]{1,0:T(8,128)(2,1)S(1)}, bf16[768,1536]{1,0:T(8,128)(2,1)S(1)}, u32[]{:S(2)}, u32[]{:S(2)}) collective-permute-start(bf16[768,1536]{1,0:T(8,128)(2,1)S(1)} %bitcast.95), channel_id=1, source_target_pairs={{0,1},{1,0},{2,3},{3,2},{4,5},{5,4},{6,7},{7,6},{8,9},{9,8},{10,11... | collective-permute-start | bytes 7077896 | tf_op jit(solution)/shard_map/ppermute | solution.py:512
  92.9 43.0 %collective-permute-start.7 = (bf16[768,768]{1,0:T(8,128)(2,1)S(1)}, bf16[768,768]{1,0:T(8,128)(2,1)S(1)}, u32[]{:S(2)}, u32[]{:S(2)}) collective-permute-start(bf16[768,768]{1,0:T(8,128)(2,1)S(1)} %copy-done.30), channel_id=1, source_target_pairs={{0,1},{1,0},{2,3},{3,2},{4,5},{5,4},{6,7},{7,6},{8,9},{9,8},{10,11... | collective-permute-start | bytes 3538952 | tf_op jit(solution)/shard_map/ppermute | solution.py:512
  111.2 50.9 %copy-start.4 = (bf16[512,768]{1,0:T(8,128)(2,1)}, bf16[512,768]{1,0:T(8,128)(2,1)S(1)}, u32[]{:S(2)}) copy-start(bf16[512,768]{1,0:T(8,128)(2,1)S(1)} %fusion.43) | copy-start | bytes 2359300
  111.2 19.1 %collective-permute-start.8 = (bf16[512,768]{1,0:T(8,128)(2,1)S(1)}, bf16[512,768]{1,0:T(8,128)(2,1)S(1)}, u32[]{:S(2)}, u32[]{:S(2)}) collective-permute-start(bf16[512,768]{1,0:T(8,128)(2,1)S(1)} %fusion.43), channel_id=1, source_target_pairs={{0,2},{1,3},{2,0},{3,1},{4,6},{5,7},{6,4},{7,5},{8,10},{9,11},{10,... | collective-permute-start | bytes 2359304 | tf_op jit(solution)/shard_map/ppermute | solution.py:512
  114.9 19.2 %copy-start.5 = (bf16[768,1536]{1,0:T(8,128)(2,1)}, bf16[768,1536]{1,0:T(8,128)(2,1)S(1)}, u32[]{:S(2)}) copy-start(bf16[768,1536]{1,0:T(8,128)(2,1)S(1)} %collective-permute-done.6) | copy-start | bytes 7077892
  130.3 47.4 %copy-start.9 = (bf16[512,768]{1,0:T(8,128)(2,1)}, bf16[512,768]{1,0:T(8,128)(2,1)S(1)}, u32[]{:S(2)}) copy-start(bf16[512,768]{1,0:T(8,128)(2,1)S(1)} %collective-permute-done.8) | copy-start | bytes 2359300
  136.8 18.2 %collective-permute-start.9 = (bf16[512,768]{1,0:T(8,128)(2,1)S(1)}, bf16[512,768]{1,0:T(8,128)(2,1)S(1)}, u32[]{:S(2)}, u32[]{:S(2)}) collective-permute-start(bf16[512,768]{1,0:T(8,128)(2,1)S(1)} %add_convert_fusion.6), channel_id=1, source_target_pairs={{0,2},{1,3},{2,0},{3,1},{4,6},{5,7},{6,4},{7,5},{8,10},{9,11},{10,... | collective-permute-start | bytes 2359304 | tf_op jit(solution)/shard_map/ppermute | solution.py:512
  158.3 17.2 %collective-permute-start.10 = (bf16[512,768]{1,0:T(8,128)(2,1)S(1)}, bf16[512,768]{1,0:T(8,128)(2,1)S(1)}, u32[]{:S(2)}, u32[]{:S(2)}) collective-permute-start(bf16[512,768]{1,0:T(8,128)(2,1)S(1)} %fusion.69), channel_id=1, source_target_pairs={{0,2},{1,3},{2,0},{3,1},{4,6},{5,7},{6,4},{7,5},{8,10},{9,11},{10,... | collective-permute-start | bytes 2359304 | tf_op jit(solution)/shard_map/ppermute | solution.py:512
  175.5 5.7 %copy-start.13 = (bf16[512,768]{1,0:T(8,128)(2,1)}, bf16[512,768]{1,0:T(8,128)(2,1)S(1)}, u32[]{:S(2)}) copy-start(bf16[512,768]{1,0:T(8,128)(2,1)S(1)} %collective-permute-done.10) | copy-start | bytes 2359300
  176.4 5.6 %collective-permute-start.17 = (bf16[768,768]{1,0:T(8,128)(2,1)S(1)}, bf16[768,768]{1,0:T(8,128)(2,1)S(1)}, u32[]{:S(2)}, u32[]{:S(2)}) collective-permute-start(bf16[768,768]{1,0:T(8,128)(2,1)S(1)} %add_convert_fusion.3), channel_id=1, source_target_pairs={{0,1},{1,0},{2,3},{3,2},{4,5},{5,4},{6,7},{7,6},{8,9},{9,8},{10,11... | collective-permute-start | bytes 3538952 | tf_op jit(solution)/shard_map/ppermute | solution.py:512
  177.7 3.0 copy-start.32
  177.7 3.0 copy-start.33
  180.7 11.8 %collective-permute-start.16 = (bf16[768,1536]{1,0:T(8,128)(2,1)}, bf16[768,1536]{1,0:T(8,128)(2,1)}, u32[]{:S(2)}, u32[]{:S(2)}) collective-permute-start(bf16[768,1536]{1,0:T(8,128)(2,1)} %add_convert_fusion.1), channel_id=1, source_target_pairs={{0,1},{1,0},{2,3},{3,2},{4,5},{5,4},{6,7},{7,6},{8,9},{9,8},{10,11... | collective-permute-start | bytes 7077896 | tf_op jit(solution)/shard_map/ppermute | solution.py:512
  183.5 137.9 %reduce-scatter.6.cloned.1.call-start = ((), (), s32[]{:S(2)}) async-start(), calls=%async_computation.4 | async-start | bytes 2654208 | tf_op jit(solution)/shard_map/reduce_scatter | solution.py:496
  183.8 3.2 copy-start.14
  183.8 3.2 copy-start.17
  183.8 3.2 copy-start.31
  188.2 1.7 copy-start.1
  197.1 258.2 %reduce-scatter.4.cloned.1.call-start = ((), (), s32[]{:S(2)}) async-start(), calls=%async_computation.3 | async-start | bytes 331776 | tf_op jit(solution)/shard_map/reduce_scatter | solution.py:496
  197.1 6.0 %copy-start.2 = (bf16[96,8,2,768]{3,1,2,0:T(8,128)(2,1)S(1)}, bf16[96,8,2,768]{3,1,2,0:T(8,128)(2,1)}, u32[]{:S(2)}) copy-start(bf16[96,8,2,768]{3,1,2,0:T(8,128)(2,1)} %copy-done) | copy-start | bytes 7077892
  197.1 6.0 %copy-start.22 = (bf16[512,768]{1,0:T(8,128)(2,1)S(1)}, bf16[512,768]{1,0:T(8,128)(2,1)}, u32[]{:S(2)}) copy-start(bf16[512,768]{1,0:T(8,128)(2,1)} %get-tuple-element.55) | copy-start | bytes 2359300
  197.2 6.0 %copy-start.23 = (bf16[512,768]{1,0:T(8,128)(2,1)S(1)}, bf16[512,768]{1,0:T(8,128)(2,1)}, u32[]{:S(2)}) copy-start(bf16[512,768]{1,0:T(8,128)(2,1)} %get-tuple-element.56) | copy-start | bytes 2359300
  201.3 3.2 copy-start.6
  201.4 3.2 copy-start.19
  201.4 3.2 copy-start.21
  201.4 19.6 %collective-permute-start.11 = (bf16[512,768]{1,0:T(8,128)(2,1)S(1)}, bf16[512,768]{1,0:T(8,128)(2,1)S(1)}, u32[]{:S(2)}, u32[]{:S(2)}) collective-permute-start(bf16[512,768]{1,0:T(8,128)(2,1)S(1)} %add_convert_fusion.4), channel_id=1, source_target_pairs={{0,2},{1,3},{2,0},{3,1},{4,6},{5,7},{6,4},{7,5},{8,10},{9,11},{10,... | collective-permute-start | bytes 2359304 | tf_op jit(solution)/shard_map/ppermute | solution.py:512
  204.6 16.4 %copy-start.8 = (bf16[512,768]{1,0:T(8,128)(2,1)S(1)}, bf16[512,768]{1,0:T(8,128)(2,1)}, u32[]{:S(2)}) copy-start(bf16[512,768]{1,0:T(8,128)(2,1)} %param.21) | copy-start | bytes 2359300
  204.6 16.4 %copy-start.28 = (f32[768]{0:T(1024)S(1)}, f32[768]{0:T(1024)}, u32[]{:S(2)}) copy-start(f32[768]{0:T(1024)} %param.20) | copy-start | bytes 9220
  225.1 18.7 %collective-permute-start.12 = (bf16[512,768]{1,0:T(8,128)(2,1)S(1)}, bf16[512,768]{1,0:T(8,128)(2,1)S(1)}, u32[]{:S(2)}, u32[]{:S(2)}) collective-permute-start(bf16[512,768]{1,0:T(8,128)(2,1)S(1)} %get-tuple-element.46), channel_id=1, source_target_pairs={{0,2},{1,3},{2,0},{3,1},{4,6},{5,7},{6,4},{7,5},{8,10},{9,11},{10,... | collective-permute-start | bytes 2359304 | tf_op jit(solution)/shard_map/ppermute | solution.py:512
  226.8 17.0 %collective-permute-start.13 = (bf16[512,768]{1,0:T(8,128)(2,1)S(1)}, bf16[512,768]{1,0:T(8,128)(2,1)S(1)}, u32[]{:S(2)}, u32[]{:S(2)}) collective-permute-start(bf16[512,768]{1,0:T(8,128)(2,1)S(1)} %get-tuple-element.46), channel_id=1, source_target_pairs={{0,1},{1,0},{2,3},{3,2},{4,5},{5,4},{6,7},{7,6},{8,9},{9,8},{10,11... | collective-permute-start | bytes 2359304 | tf_op jit(solution)/shard_map/ppermute | solution.py:512
  243.8 2.3 collective-permute-start.14
  247.3 1.8 copy-start.3
  249.1 239.1 %all-gather.5.cloned.1.call-start = ((), (), s32[]{:S(2)}) async-start(), calls=%async_computation.7 | async-start | bytes 1327104 | tf_op jit(solution)/shard_map/all_gather | solution.py:497
  249.9 241.2 %all-gather.3.cloned.1.call-start = ((), (), s32[]{:S(2)}) async-start(), calls=%async_computation.5 | async-start | bytes 2654208 | tf_op jit(solution)/shard_map/all_gather | solution.py:497
  321.4 2.7 collective-permute-start.15
  491.1 6.3 %copy-start.24 = (bf16[512,768]{1,0:T(8,128)(2,1)S(1)}, bf16[512,768]{1,0:T(8,128)(2,1)}, u32[]{:S(2)}) copy-start(bf16[512,768]{1,0:T(8,128)(2,1)} %get-tuple-element.93) | copy-start | bytes 2359300
  (9 other events, 10.3 us)
Sparse Core Ops, SparseCore 0:
  183.6 66.2 reduce-scatter.7
  253.4 67.9 reduce-scatter.5
  325.2 57.7 reduce-scatter.3
  385.1 48.4 all-gather.4
  435.6 53.1 all-gather.2
